TPU v7x, 256 devices: a whole 4x4x8 slice. The times are simulated.
256 devices in a mesh: ctx: 32 (over y, x, core), head: 8 (over z).
Axes of the slice: x: 4, y: 4, z: 8, core: 2. Of those that a mesh axis runs over, the one named last changes fastest.
Arguments:
- queries: bfloat16 [4096, 1024], P('ctx', 'head'), may hold values from -6 to 6
- key_vectors: bfloat16 [4096, 1024], P('ctx', 'head'), may hold values from -6 to 6
- value_rows: bfloat16 [4096, 2048], P('ctx', 'head'), may hold values from -6 to 6
- write_rate: float32 [16, 4096], P('head', 'ctx'), may hold values from 0.001953125 to 1
- log_decay: float32 [16, 4096], P('head', 'ctx'), may hold values from -0.9 to 0
- doc_offsets: int32 [5], replicated, may hold values from 0 to 4096, as said below
- out_weight: bfloat16 [2048, 2048], P('head'), may hold values from -0.125 to 0.125
- grad_out: bfloat16 [4096, 2048], P(('ctx', 'head')), may hold values from -24 to 24
Outputs:
- layer_out: float32 [4096, 2048], P(('ctx', 'head'))
- grad_q: float32 [4096, 1024], P('ctx', 'head')
- grad_k: float32 [4096, 1024], P('ctx', 'head')
- grad_v: float32 [4096, 2048], P('ctx', 'head')
- grad_rate: float32 [16, 4096], P('head', 'ctx')
- grad_decay: float32 [16, 4096], P('head', 'ctx')
- weight_grad: float32 [2048, 2048], P('ctx', 'head')
Inputs may be any that keep to these rules, and one draw needn't show every extreme that they name: `doc_offsets`: Increasing; the first entry is 0 and the last is 4096.
All inputs are finite; a program needn't handle non-finite values.
Results may differ from a plain program's by a relative error of at most 0.0029.
Values may be sent and summed in bfloat16 or wider, within the bound.
A program may use at most 64 MiB of HBM per device.

v0:
```python
from functools import partial

import jax
import jax.numpy as jnp
from jax import lax
from jax.sharding import PartitionSpec as P

DK = 128
DV = 128
STRETCH = 64


full_precision = lax.Precision.HIGHEST


def shifted(value, axis, by):
    length = lax.axis_size(axis)
    pairs = [(i, i + by) for i in range(length) if 0 <= i + by < length]
    return lax.ppermute(value, axis, pairs)


def tri_inverse(strict_lower):
    order_size = strict_lower.shape[-1]
    identity = jnp.eye(order_size, dtype=strict_lower.dtype)
    powers = -strict_lower
    result = identity + powers
    reach_span = 2
    while reach_span < order_size:
        powers = jnp.einsum("hij,hjk->hik", powers, powers, precision=full_precision)
        result = jnp.einsum("hij,hjk->hik", result, identity + powers, precision=full_precision)
        reach_span = reach_span * 2
    return result


def block_step(state, inputs):
    query_blk, key_blk, value_blk, rate_blk, decay_blk, reset_blk = inputs
    dtype_f = decay_blk.dtype
    cumul = jnp.cumsum(decay_blk, axis=-1)
    segment = jnp.cumsum(reset_blk)
    block_len = reset_blk.shape[0]
    row_ids = lax.broadcasted_iota(jnp.int32, (block_len, block_len), 0)
    col_ids = lax.broadcasted_iota(jnp.int32, (block_len, block_len), 1)
    same_seg = segment[:, None] == segment[None, :]
    together = same_seg & (row_ids >= col_ids)
    strict = same_seg & (row_ids > col_ids)
    gaps = cumul[:, :, None] - cumul[:, None, :]
    ratio = jnp.exp(jnp.where(together, gaps, 0.0)) * together.astype(dtype_f)
    from_start = jnp.exp(cumul) * (segment == 0).astype(dtype_f)
    to_end = jnp.exp(cumul[:, -1:] - cumul) * (segment == segment[-1]).astype(dtype_f)
    whole_decay = jnp.exp(cumul[:, -1]) * (segment[-1] == 0).astype(dtype_f)
    key_dots = jnp.einsum("hik,hjk->hij", key_blk, key_blk, precision=full_precision)
    coupling = rate_blk[:, :, None] * key_dots * ratio * strict.astype(dtype_f)
    inverse = tri_inverse(coupling)
    right_side = jnp.concatenate(
        [rate_blk[:, :, None] * value_blk, (rate_blk * from_start)[:, :, None] * key_blk], axis=-1
    )
    solved = jnp.einsum("hij,hjw->hiw", inverse, right_side, precision=full_precision)
    value_width = value_blk.shape[-1]
    pseudo = solved[..., :value_width] - jnp.einsum(
        "hck,hvk->hcv", solved[..., value_width:], state, precision=full_precision
    )
    scores = jnp.einsum("hik,hjk->hij", query_blk, key_blk, precision=full_precision) * ratio
    outputs = from_start[:, :, None] * jnp.einsum(
        "hck,hvk->hcv", query_blk, state, precision=full_precision
    )
    outputs = outputs + jnp.einsum("hij,hjv->hiv", scores, pseudo, precision=full_precision)
    new_state = whole_decay[:, None, None] * state + jnp.einsum(
        "hcv,hck->hvk", pseudo, to_end[:, :, None] * key_blk, precision=full_precision
    )
    return (new_state, outputs)


def run_blocks(state, query_heads, key_heads, value_heads, rates, decays, resets, block_size):
    head_count, length = rates.shape
    blocks = length // block_size

    def split_rows(tensor):
        return jnp.moveaxis(tensor.reshape(head_count, blocks, block_size, tensor.shape[-1]), 1, 0)

    stacked = (
        split_rows(query_heads),
        split_rows(key_heads),
        split_rows(value_heads),
        jnp.moveaxis(rates.reshape(head_count, blocks, block_size), 1, 0),
        jnp.moveaxis(decays.reshape(head_count, blocks, block_size), 1, 0),
        resets.reshape(blocks, block_size),
    )
    final_state, outputs = lax.scan(jax.checkpoint(block_step), state, stacked)
    outputs = jnp.moveaxis(outputs, 0, 1).reshape(head_count, length, outputs.shape[-1])
    return (final_state, outputs)


def to_heads(query_f, key_f, value_f):
    length = query_f.shape[0]

    def heads_first(tensor, width):
        return jnp.transpose(tensor.reshape(length, tensor.shape[1] // width, width), (1, 0, 2))

    def unit_rows(tensor):
        return tensor / jnp.sqrt(jnp.sum(tensor * tensor, axis=-1, keepdims=True) + 1e-06)

    value_heads = heads_first(value_f, DV)
    repeat_by = value_heads.shape[0] // (key_f.shape[1] // DK)
    query_heads = jnp.repeat(unit_rows(heads_first(query_f, DK)), repeat_by, axis=0)
    key_heads = jnp.repeat(unit_rows(heads_first(key_f, DK)), repeat_by, axis=0)
    return (query_heads, key_heads, value_heads)


def local_pass(query_f, key_f, value_f, rates, decays, resets):
    query_heads, key_heads, value_heads = to_heads(query_f, key_f, value_f)
    head_count, length, value_width = value_heads.shape
    key_width = key_heads.shape[-1]
    padded_values = jnp.concatenate(
        [value_heads, jnp.zeros((head_count, length, key_width), value_f.dtype)], axis=-1
    )
    start_state = jnp.concatenate(
        [
            jnp.zeros((head_count, value_width, key_width), value_f.dtype),
            jnp.broadcast_to(
                jnp.eye(key_width, dtype=value_f.dtype), (head_count, key_width, key_width)
            ),
        ],
        axis=1,
    )
    final_state, outputs = run_blocks(
        start_state, query_heads, key_heads, padded_values, rates, decays, resets, STRETCH
    )
    return (
        outputs[..., :value_width],
        outputs[..., value_width:],
        final_state[:, value_width:, :],
        final_state[:, :value_width, :],
    )


def forward_chain(transfer, local_state):
    steps_total = lax.axis_size("ctx") - 1

    def forward_advance(step_index, carry_pair):
        incoming, outgoing = carry_pair
        incoming = shifted(outgoing, "ctx", 1)
        outgoing = (
            jnp.einsum("hvk,hkj->hvj", incoming, transfer, precision=full_precision) + local_state
        )
        return (incoming, outgoing)

    zero_state = jnp.zeros_like(local_state)
    incoming, outgoing = lax.fori_loop(0, steps_total, forward_advance, (zero_state, local_state))
    return incoming


def backward_chain(transfer, adjoint_local):
    steps_total = lax.axis_size("ctx") - 1

    def backward_advance(step_index, carry_pair):
        received, outgoing = carry_pair
        received = shifted(outgoing, "ctx", -1)
        outgoing = (
            jnp.einsum("hvk,hjk->hvj", received, transfer, precision=full_precision) + adjoint_local
        )
        return (received, outgoing)

    zero_state = jnp.zeros_like(adjoint_local)
    received, outgoing = lax.fori_loop(
        0, steps_total, backward_advance, (zero_state, adjoint_local)
    )
    return received


def per_device(
    queries, key_vectors, value_rows, write_rate, log_decay, doc_offsets, out_weight, grad_out
):
    tok_count = queries.shape[0]
    shard_start = lax.axis_index("ctx") * tok_count
    positions = shard_start + lax.broadcasted_iota(jnp.int32, (tok_count,), 0)
    resets = jnp.any(positions[:, None] == doc_offsets[None, :-1], axis=1).astype(jnp.int32)
    full_grad = lax.all_gather(grad_out, "head", axis=0, tiled=True)
    d_core = jnp.einsum("td,cd->tc", full_grad, out_weight, preferred_element_type=jnp.float32)
    head_count = write_rate.shape[0]
    d_heads = jnp.transpose(d_core.reshape(tok_count, head_count, DV), (1, 0, 2))
    pass_out, pass_vjp = jax.vjp(
        partial(local_pass, resets=resets),
        queries.astype(jnp.float32),
        key_vectors.astype(jnp.float32),
        value_rows.astype(jnp.float32),
        write_rate,
        log_decay,
    )
    o_local, q_tilde, transfer, local_state = pass_out
    adjoint_local = jnp.einsum("htv,htk->hvk", d_heads, q_tilde, precision=full_precision)
    incoming = forward_chain(transfer, local_state)
    adjoint_out = backward_chain(transfer, adjoint_local)
    core_heads = o_local + jnp.einsum("htk,hvk->htv", q_tilde, incoming, precision=full_precision)
    mixed_in = (
        jnp.transpose(core_heads, (1, 0, 2))
        .reshape(tok_count, head_count * DV)
        .astype(jnp.bfloat16)
    )
    layer_out = lax.psum_scatter(
        jnp.dot(mixed_in, out_weight, preferred_element_type=jnp.float32),
        "head",
        scatter_dimension=0,
        tiled=True,
    )
    weight_grad = lax.psum_scatter(
        jnp.einsum("td,tc->dc", full_grad, mixed_in, preferred_element_type=jnp.float32),
        "ctx",
        scatter_dimension=0,
        tiled=True,
    )
    d_qtilde = jnp.einsum("htv,hvk->htk", d_heads, incoming, precision=full_precision)
    d_transfer = jnp.einsum("hvk,hvj->hkj", incoming, adjoint_out, precision=full_precision)
    all_grads = pass_vjp((d_heads, d_qtilde, d_transfer, adjoint_out))
    grad_q, grad_k, grad_v, grad_rate, grad_decay = all_grads
    return (layer_out, grad_q, grad_k, grad_v, grad_rate, grad_decay, weight_grad)


def solution(mesh):
    placed = (
        P("ctx", "head"),
        P("ctx", "head"),
        P("ctx", "head"),
        P("head", "ctx"),
        P("head", "ctx"),
        P(),
        P("head", None),
        P(("ctx", "head"), None),
    )
    return jax.shard_map(
        per_device,
        mesh=mesh,
        in_specs=placed,
        out_specs=(
            P(("ctx", "head"), None),
            P("ctx", "head"),
            P("ctx", "head"),
            P("ctx", "head"),
            P("head", "ctx"),
            P("head", "ctx"),
            P("ctx", "head"),
        ),
        check_vma=False,
    )
```

profile of v0, /device:TPU:15, one launch (start us, length us, event | category | flops | bytes accessed | tf_op | source)
XLA Modules:
  0.0 714.7 jit_solution(8941396087570297310)
XLA Ops:
  15.6 16.6 %while.69 = (s32[]{:T(128)}, f32[2,256,128]{2,1,0:T(8,128)S(1)}, f32[2,2,64,256]{3,2,1,0:T(8,128)S(1)}, f32[2,2,256,128]{3,2,1,0:T(8,128)}, f32[2,2,64]{2,1,0:T(...) while((s32[]{:T(128)}, f32[2,256,128]{2,1,0:T(8,128)S(1)}, ...), condition=%wide.region_6.7_spmd.clone.clone, body=%wide.region_3.6_spmd.clone.clone.sunk | while | flops 302522944 | bytes 4921599 | solution.py:88
  32.9 277.5 %while.66 = (s32[]{:T(128)}, f32[2,128,128]{2,1,0:T(8,128)}, f32[2,128,128]{2,1,0:T(8,128)S(1)}, f32[2,128,128]{2,1,0:T(8,128)S(1)}, f32[2,128,128]{2,1,0:T(8,128)S(1)}, /*index=5*/s32[]{:T(128)}) while((s32[]{:T(128)}, f32[2,128,128]{2,1,0:T(8,128)}, f32[2,128,128]{2,1,0:T(8,128)S(1)}, f32[2,128,128]{2,1,0:T(8,128)S(1)}, ...), condition=%wide.region_8.9_spmd, body=%wide.region_7.8_spmd.sunk | while | flops 50364416 | bytes 1573001 | solution.py:148
  39.2 6.5 collective-permute-start
  48.2 6.5 collective-permute-start
  57.3 6.5 collective-permute-start
  66.3 6.5 collective-permute-start
  75.3 6.5 collective-permute-start
  84.4 6.5 collective-permute-start
  93.4 6.5 collective-permute-start
  102.5 6.5 collective-permute-start
  111.5 6.5 collective-permute-start
  120.5 6.5 collective-permute-start
  129.6 6.5 collective-permute-start
  138.6 6.5 collective-permute-start
  147.7 6.5 collective-permute-start
  156.7 6.5 collective-permute-start
  165.7 6.5 collective-permute-start
  174.8 6.5 collective-permute-start
  183.8 6.5 collective-permute-start
  192.9 6.5 collective-permute-start
  201.9 6.5 collective-permute-start
  210.9 6.5 collective-permute-start
  220.0 6.5 collective-permute-start
  229.0 6.5 collective-permute-start
  238.1 6.5 collective-permute-start
  247.1 6.5 collective-permute-start
  265.2 6.5 collective-permute-start
  274.2 6.5 collective-permute-start
  292.3 6.5 collective-permute-start
  301.3 6.5 collective-permute-start
  313.3 23.8 %all_gather.3 = bf16[128,2048]{1,0:T(8,128)(2,1)S(1)} all-gather(bf16[16,2048]{1,0:T(8,128)(2,1)S(1)} %copy-done.26), channel_id=1, replica_groups=mesh['ctx'=32,'head'=8] {'head'}, dimensions={0}, use_global_device_ids=true | all-gather | bytes 589824 | tf_op jit(solution)/shard_map/all_gather | solution.py:177
  343.6 288.7 %while.67 = (s32[]{:T(128)}, f32[2,128,128]{2,1,0:T(8,128)}, f32[2,128,128]{2,1,0:T(8,128)S(1)}, f32[2,128,128]{2,1,0:T(8,128)S(1)}, f32[2,128,128]{2,1,0:T(8,128)S(1)}, /*index=5*/s32[]{:T(128)}) while((s32[]{:T(128)}, f32[2,128,128]{2,1,0:T(8,128)}, f32[2,128,128]{2,1,0:T(8,128)S(1)}, f32[2,128,128]{2,1,0:T(8,128)S(1)}, ...), condition=%wide.region_11.12_spmd, body=%wide.region_10.11_spmd.sunk | while | flops 50364416 | bytes 1573001 | solution.py:164
  346.1 12.6 %collective-permute-done.1 = f32[2,128,128]{2,1,0:T(8,128)S(1)} collective-permute-done((f32[2,128,128]{2,1,0:T(8,128)S(1)}, f32[2,128,128]{2,1,0:T(8,128)S(1)}, u32[]{:S(2)}, u32[]{:S(2)}) %collective-permute-start.1) | collective-permute-done | bytes 131104 | tf_op jit(solution)/shard_map/while/body/eval_jaxpr/ppermute | solution.py:19
  361.2 6.5 collective-permute-done.1
  370.3 6.5 collective-permute-done.1
  379.3 6.5 collective-permute-done.1
  388.3 6.5 collective-permute-done.1
  397.4 6.5 collective-permute-done.1
  406.4 7.9 %collective-permute-done.1 = f32[2,128,128]{2,1,0:T(8,128)S(1)} collective-permute-done((f32[2,128,128]{2,1,0:T(8,128)S(1)}, f32[2,128,128]{2,1,0:T(8,128)S(1)}, u32[]{:S(2)}, u32[]{:S(2)}) %collective-permute-start.1) | collective-permute-done | bytes 131104 | tf_op jit(solution)/shard_map/while/body/eval_jaxpr/ppermute | solution.py:19
  416.9 6.6 collective-permute-done.1
  426.1 6.5 collective-permute-done.1
  435.1 6.7 collective-permute-done.1
  444.4 6.5 collective-permute-done.1
  453.5 6.5 collective-permute-done.1
  462.5 6.5 collective-permute-done.1
  471.6 6.5 collective-permute-done.1
  480.6 6.5 collective-permute-done.1
  489.6 6.5 collective-permute-done.1
  498.7 6.5 collective-permute-done.1
  507.7 6.5 collective-permute-done.1
  516.8 6.5 collective-permute-done.1
  525.8 6.5 collective-permute-done.1
  534.8 6.5 collective-permute-done.1
  543.9 6.5 collective-permute-done.1
  552.9 6.5 collective-permute-done.1
  562.0 6.5 collective-permute-done.1
  571.0 6.5 collective-permute-done.1
  580.0 6.5 collective-permute-done.1
  589.1 6.5 collective-permute-done.1
  598.1 6.5 collective-permute-done.1
  607.2 6.5 collective-permute-done.1
  616.2 6.5 collective-permute-done.1
  625.2 6.5 collective-permute-done.1
  638.5 58.4 %while.68 = (s32[]{:T(128)}, f32[2,256,128]{2,1,0:T(8,128)S(1)}, f32[2,2,64,128]{3,2,1,0:T(8,128)}, f32[2,2,64,128]{3,2,1,0:T(8,128)}, f32[2,2,64,256]{3,2,0,1:T...) while((s32[]{:T(128)}, f32[2,256,128]{2,1,0:T(8,128)S(1)}, ...), condition=%wide.region_25.26_spmd, body=%wide.region_12.0_spmd.sunk | while | flops 832210880 | bytes 18997520 | solution.py:88
  (672 shorter events, 281.9 us)
Async XLA Ops:
  7.2 700.7 %reduce-scatter.5.cloned.1.call-start = ((), (), s32[]{:S(2)}) async-start(), calls=%async_computation.2 | async-start | bytes 1179648 | tf_op jit(solution)/shard_map/reduce_scatter | solution.py:199
  32.9 5.6 collective-permute-start
  39.2 8.4 %collective-permute-start = (f32[2,128,128]{2,1,0:T(8,128)S(1)}, f32[2,128,128]{2,1,0:T(8,128)S(1)}, u32[]{:S(2)}, u32[]{:S(2)}) collective-permute-start(f32[2,128,128]{2,1,0:T(8,128)S(1)} %get-tuple-element.1212), channel_id=1, source_target_pairs={{0,8},{8,16},{16,24},{24,32},{32,40},{40,48},{48,56},{56,64},{64,7... | collective-permute-start | bytes 393224 | tf_op jit(solution)/shard_map/while/body/eval_jaxpr/ppermute | solution.py:19
  48.2 8.4 %collective-permute-start = (f32[2,128,128]{2,1,0:T(8,128)S(1)}, f32[2,128,128]{2,1,0:T(8,128)S(1)}, u32[]{:S(2)}, u32[]{:S(2)}) collective-permute-start(f32[2,128,128]{2,1,0:T(8,128)S(1)} %get-tuple-element.1212), channel_id=1, source_target_pairs={{0,8},{8,16},{16,24},{24,32},{32,40},{40,48},{48,56},{56,64},{64,7... | collective-permute-start | bytes 393224 | tf_op jit(solution)/shard_map/while/body/eval_jaxpr/ppermute | solution.py:19
  57.3 8.4 %collective-permute-start = (f32[2,128,128]{2,1,0:T(8,128)S(1)}, f32[2,128,128]{2,1,0:T(8,128)S(1)}, u32[]{:S(2)}, u32[]{:S(2)}) collective-permute-start(f32[2,128,128]{2,1,0:T(8,128)S(1)} %get-tuple-element.1212), channel_id=1, source_target_pairs={{0,8},{8,16},{16,24},{24,32},{32,40},{40,48},{48,56},{56,64},{64,7... | collective-permute-start | bytes 393224 | tf_op jit(solution)/shard_map/while/body/eval_jaxpr/ppermute | solution.py:19
  66.3 8.4 %collective-permute-start = (f32[2,128,128]{2,1,0:T(8,128)S(1)}, f32[2,128,128]{2,1,0:T(8,128)S(1)}, u32[]{:S(2)}, u32[]{:S(2)}) collective-permute-start(f32[2,128,128]{2,1,0:T(8,128)S(1)} %get-tuple-element.1212), channel_id=1, source_target_pairs={{0,8},{8,16},{16,24},{24,32},{32,40},{40,48},{48,56},{56,64},{64,7... | collective-permute-start | bytes 393224 | tf_op jit(solution)/shard_map/while/body/eval_jaxpr/ppermute | solution.py:19
  75.3 8.4 %collective-permute-start = (f32[2,128,128]{2,1,0:T(8,128)S(1)}, f32[2,128,128]{2,1,0:T(8,128)S(1)}, u32[]{:S(2)}, u32[]{:S(2)}) collective-permute-start(f32[2,128,128]{2,1,0:T(8,128)S(1)} %get-tuple-element.1212), channel_id=1, source_target_pairs={{0,8},{8,16},{16,24},{24,32},{32,40},{40,48},{48,56},{56,64},{64,7... | collective-permute-start | bytes 393224 | tf_op jit(solution)/shard_map/while/body/eval_jaxpr/ppermute | solution.py:19
  84.4 8.4 %collective-permute-start = (f32[2,128,128]{2,1,0:T(8,128)S(1)}, f32[2,128,128]{2,1,0:T(8,128)S(1)}, u32[]{:S(2)}, u32[]{:S(2)}) collective-permute-start(f32[2,128,128]{2,1,0:T(8,128)S(1)} %get-tuple-element.1212), channel_id=1, source_target_pairs={{0,8},{8,16},{16,24},{24,32},{32,40},{40,48},{48,56},{56,64},{64,7... | collective-permute-start | bytes 393224 | tf_op jit(solution)/shard_map/while/body/eval_jaxpr/ppermute | solution.py:19
  93.4 8.4 %collective-permute-start = (f32[2,128,128]{2,1,0:T(8,128)S(1)}, f32[2,128,128]{2,1,0:T(8,128)S(1)}, u32[]{:S(2)}, u32[]{:S(2)}) collective-permute-start(f32[2,128,128]{2,1,0:T(8,128)S(1)} %get-tuple-element.1212), channel_id=1, source_target_pairs={{0,8},{8,16},{16,24},{24,32},{32,40},{40,48},{48,56},{56,64},{64,7... | collective-permute-start | bytes 393224 | tf_op jit(solution)/shard_map/while/body/eval_jaxpr/ppermute | solution.py:19
  102.5 8.4 %collective-permute-start = (f32[2,128,128]{2,1,0:T(8,128)S(1)}, f32[2,128,128]{2,1,0:T(8,128)S(1)}, u32[]{:S(2)}, u32[]{:S(2)}) collective-permute-start(f32[2,128,128]{2,1,0:T(8,128)S(1)} %get-tuple-element.1212), channel_id=1, source_target_pairs={{0,8},{8,16},{16,24},{24,32},{32,40},{40,48},{48,56},{56,64},{64,7... | collective-permute-start | bytes 393224 | tf_op jit(solution)/shard_map/while/body/eval_jaxpr/ppermute | solution.py:19
  111.5 8.4 %collective-permute-start = (f32[2,128,128]{2,1,0:T(8,128)S(1)}, f32[2,128,128]{2,1,0:T(8,128)S(1)}, u32[]{:S(2)}, u32[]{:S(2)}) collective-permute-start(f32[2,128,128]{2,1,0:T(8,128)S(1)} %get-tuple-element.1212), channel_id=1, source_target_pairs={{0,8},{8,16},{16,24},{24,32},{32,40},{40,48},{48,56},{56,64},{64,7... | collective-permute-start | bytes 393224 | tf_op jit(solution)/shard_map/while/body/eval_jaxpr/ppermute | solution.py:19
  120.5 8.4 %collective-permute-start = (f32[2,128,128]{2,1,0:T(8,128)S(1)}, f32[2,128,128]{2,1,0:T(8,128)S(1)}, u32[]{:S(2)}, u32[]{:S(2)}) collective-permute-start(f32[2,128,128]{2,1,0:T(8,128)S(1)} %get-tuple-element.1212), channel_id=1, source_target_pairs={{0,8},{8,16},{16,24},{24,32},{32,40},{40,48},{48,56},{56,64},{64,7... | collective-permute-start | bytes 393224 | tf_op jit(solution)/shard_map/while/body/eval_jaxpr/ppermute | solution.py:19
  129.6 8.4 %collective-permute-start = (f32[2,128,128]{2,1,0:T(8,128)S(1)}, f32[2,128,128]{2,1,0:T(8,128)S(1)}, u32[]{:S(2)}, u32[]{:S(2)}) collective-permute-start(f32[2,128,128]{2,1,0:T(8,128)S(1)} %get-tuple-element.1212), channel_id=1, source_target_pairs={{0,8},{8,16},{16,24},{24,32},{32,40},{40,48},{48,56},{56,64},{64,7... | collective-permute-start | bytes 393224 | tf_op jit(solution)/shard_map/while/body/eval_jaxpr/ppermute | solution.py:19
  138.6 8.4 %collective-permute-start = (f32[2,128,128]{2,1,0:T(8,128)S(1)}, f32[2,128,128]{2,1,0:T(8,128)S(1)}, u32[]{:S(2)}, u32[]{:S(2)}) collective-permute-start(f32[2,128,128]{2,1,0:T(8,128)S(1)} %get-tuple-element.1212), channel_id=1, source_target_pairs={{0,8},{8,16},{16,24},{24,32},{32,40},{40,48},{48,56},{56,64},{64,7... | collective-permute-start | bytes 393224 | tf_op jit(solution)/shard_map/while/body/eval_jaxpr/ppermute | solution.py:19
  147.7 8.4 %collective-permute-start = (f32[2,128,128]{2,1,0:T(8,128)S(1)}, f32[2,128,128]{2,1,0:T(8,128)S(1)}, u32[]{:S(2)}, u32[]{:S(2)}) collective-permute-start(f32[2,128,128]{2,1,0:T(8,128)S(1)} %get-tuple-element.1212), channel_id=1, source_target_pairs={{0,8},{8,16},{16,24},{24,32},{32,40},{40,48},{48,56},{56,64},{64,7... | collective-permute-start | bytes 393224 | tf_op jit(solution)/shard_map/while/body/eval_jaxpr/ppermute | solution.py:19
  156.7 8.4 %collective-permute-start = (f32[2,128,128]{2,1,0:T(8,128)S(1)}, f32[2,128,128]{2,1,0:T(8,128)S(1)}, u32[]{:S(2)}, u32[]{:S(2)}) collective-permute-start(f32[2,128,128]{2,1,0:T(8,128)S(1)} %get-tuple-element.1212), channel_id=1, source_target_pairs={{0,8},{8,16},{16,24},{24,32},{32,40},{40,48},{48,56},{56,64},{64,7... | collective-permute-start | bytes 393224 | tf_op jit(solution)/shard_map/while/body/eval_jaxpr/ppermute | solution.py:19
  165.7 8.4 %collective-permute-start = (f32[2,128,128]{2,1,0:T(8,128)S(1)}, f32[2,128,128]{2,1,0:T(8,128)S(1)}, u32[]{:S(2)}, u32[]{:S(2)}) collective-permute-start(f32[2,128,128]{2,1,0:T(8,128)S(1)} %get-tuple-element.1212), channel_id=1, source_target_pairs={{0,8},{8,16},{16,24},{24,32},{32,40},{40,48},{48,56},{56,64},{64,7... | collective-permute-start | bytes 393224 | tf_op jit(solution)/shard_map/while/body/eval_jaxpr/ppermute | solution.py:19
  174.8 8.4 %collective-permute-start = (f32[2,128,128]{2,1,0:T(8,128)S(1)}, f32[2,128,128]{2,1,0:T(8,128)S(1)}, u32[]{:S(2)}, u32[]{:S(2)}) collective-permute-start(f32[2,128,128]{2,1,0:T(8,128)S(1)} %get-tuple-element.1212), channel_id=1, source_target_pairs={{0,8},{8,16},{16,24},{24,32},{32,40},{40,48},{48,56},{56,64},{64,7... | collective-permute-start | bytes 393224 | tf_op jit(solution)/shard_map/while/body/eval_jaxpr/ppermute | solution.py:19
  183.8 8.4 %collective-permute-start = (f32[2,128,128]{2,1,0:T(8,128)S(1)}, f32[2,128,128]{2,1,0:T(8,128)S(1)}, u32[]{:S(2)}, u32[]{:S(2)}) collective-permute-start(f32[2,128,128]{2,1,0:T(8,128)S(1)} %get-tuple-element.1212), channel_id=1, source_target_pairs={{0,8},{8,16},{16,24},{24,32},{32,40},{40,48},{48,56},{56,64},{64,7... | collective-permute-start | bytes 393224 | tf_op jit(solution)/shard_map/while/body/eval_jaxpr/ppermute | solution.py:19
  192.9 8.4 %collective-permute-start = (f32[2,128,128]{2,1,0:T(8,128)S(1)}, f32[2,128,128]{2,1,0:T(8,128)S(1)}, u32[]{:S(2)}, u32[]{:S(2)}) collective-permute-start(f32[2,128,128]{2,1,0:T(8,128)S(1)} %get-tuple-element.1212), channel_id=1, source_target_pairs={{0,8},{8,16},{16,24},{24,32},{32,40},{40,48},{48,56},{56,64},{64,7... | collective-permute-start | bytes 393224 | tf_op jit(solution)/shard_map/while/body/eval_jaxpr/ppermute | solution.py:19
  201.9 8.4 %collective-permute-start = (f32[2,128,128]{2,1,0:T(8,128)S(1)}, f32[2,128,128]{2,1,0:T(8,128)S(1)}, u32[]{:S(2)}, u32[]{:S(2)}) collective-permute-start(f32[2,128,128]{2,1,0:T(8,128)S(1)} %get-tuple-element.1212), channel_id=1, source_target_pairs={{0,8},{8,16},{16,24},{24,32},{32,40},{40,48},{48,56},{56,64},{64,7... | collective-permute-start | bytes 393224 | tf_op jit(solution)/shard_map/while/body/eval_jaxpr/ppermute | solution.py:19
  210.9 8.4 %collective-permute-start = (f32[2,128,128]{2,1,0:T(8,128)S(1)}, f32[2,128,128]{2,1,0:T(8,128)S(1)}, u32[]{:S(2)}, u32[]{:S(2)}) collective-permute-start(f32[2,128,128]{2,1,0:T(8,128)S(1)} %get-tuple-element.1212), channel_id=1, source_target_pairs={{0,8},{8,16},{16,24},{24,32},{32,40},{40,48},{48,56},{56,64},{64,7... | collective-permute-start | bytes 393224 | tf_op jit(solution)/shard_map/while/body/eval_jaxpr/ppermute | solution.py:19
  220.0 8.4 %collective-permute-start = (f32[2,128,128]{2,1,0:T(8,128)S(1)}, f32[2,128,128]{2,1,0:T(8,128)S(1)}, u32[]{:S(2)}, u32[]{:S(2)}) collective-permute-start(f32[2,128,128]{2,1,0:T(8,128)S(1)} %get-tuple-element.1212), channel_id=1, source_target_pairs={{0,8},{8,16},{16,24},{24,32},{32,40},{40,48},{48,56},{56,64},{64,7... | collective-permute-start | bytes 393224 | tf_op jit(solution)/shard_map/while/body/eval_jaxpr/ppermute | solution.py:19
  229.0 8.4 %collective-permute-start = (f32[2,128,128]{2,1,0:T(8,128)S(1)}, f32[2,128,128]{2,1,0:T(8,128)S(1)}, u32[]{:S(2)}, u32[]{:S(2)}) collective-permute-start(f32[2,128,128]{2,1,0:T(8,128)S(1)} %get-tuple-element.1212), channel_id=1, source_target_pairs={{0,8},{8,16},{16,24},{24,32},{32,40},{40,48},{48,56},{56,64},{64,7... | collective-permute-start | bytes 393224 | tf_op jit(solution)/shard_map/while/body/eval_jaxpr/ppermute | solution.py:19
  238.1 8.4 %collective-permute-start = (f32[2,128,128]{2,1,0:T(8,128)S(1)}, f32[2,128,128]{2,1,0:T(8,128)S(1)}, u32[]{:S(2)}, u32[]{:S(2)}) collective-permute-start(f32[2,128,128]{2,1,0:T(8,128)S(1)} %get-tuple-element.1212), channel_id=1, source_target_pairs={{0,8},{8,16},{16,24},{24,32},{32,40},{40,48},{48,56},{56,64},{64,7... | collective-permute-start | bytes 393224 | tf_op jit(solution)/shard_map/while/body/eval_jaxpr/ppermute | solution.py:19
  247.1 8.4 %collective-permute-start = (f32[2,128,128]{2,1,0:T(8,128)S(1)}, f32[2,128,128]{2,1,0:T(8,128)S(1)}, u32[]{:S(2)}, u32[]{:S(2)}) collective-permute-start(f32[2,128,128]{2,1,0:T(8,128)S(1)} %get-tuple-element.1212), channel_id=1, source_target_pairs={{0,8},{8,16},{16,24},{24,32},{32,40},{40,48},{48,56},{56,64},{64,7... | collective-permute-start | bytes 393224 | tf_op jit(solution)/shard_map/while/body/eval_jaxpr/ppermute | solution.py:19
  256.1 8.4 %collective-permute-start = (f32[2,128,128]{2,1,0:T(8,128)S(1)}, f32[2,128,128]{2,1,0:T(8,128)S(1)}, u32[]{:S(2)}, u32[]{:S(2)}) collective-permute-start(f32[2,128,128]{2,1,0:T(8,128)S(1)} %get-tuple-element.1212), channel_id=1, source_target_pairs={{0,8},{8,16},{16,24},{24,32},{32,40},{40,48},{48,56},{56,64},{64,7... | collective-permute-start | bytes 393224 | tf_op jit(solution)/shard_map/while/body/eval_jaxpr/ppermute | solution.py:19
  265.2 8.4 %collective-permute-start = (f32[2,128,128]{2,1,0:T(8,128)S(1)}, f32[2,128,128]{2,1,0:T(8,128)S(1)}, u32[]{:S(2)}, u32[]{:S(2)}) collective-permute-start(f32[2,128,128]{2,1,0:T(8,128)S(1)} %get-tuple-element.1212), channel_id=1, source_target_pairs={{0,8},{8,16},{16,24},{24,32},{32,40},{40,48},{48,56},{56,64},{64,7... | collective-permute-start | bytes 393224 | tf_op jit(solution)/shard_map/while/body/eval_jaxpr/ppermute | solution.py:19
  274.2 8.4 %collective-permute-start = (f32[2,128,128]{2,1,0:T(8,128)S(1)}, f32[2,128,128]{2,1,0:T(8,128)S(1)}, u32[]{:S(2)}, u32[]{:S(2)}) collective-permute-start(f32[2,128,128]{2,1,0:T(8,128)S(1)} %get-tuple-element.1212), channel_id=1, source_target_pairs={{0,8},{8,16},{16,24},{24,32},{32,40},{40,48},{48,56},{56,64},{64,7... | collective-permute-start | bytes 393224 | tf_op jit(solution)/shard_map/while/body/eval_jaxpr/ppermute | solution.py:19
  283.3 8.4 %collective-permute-start = (f32[2,128,128]{2,1,0:T(8,128)S(1)}, f32[2,128,128]{2,1,0:T(8,128)S(1)}, u32[]{:S(2)}, u32[]{:S(2)}) collective-permute-start(f32[2,128,128]{2,1,0:T(8,128)S(1)} %get-tuple-element.1212), channel_id=1, source_target_pairs={{0,8},{8,16},{16,24},{24,32},{32,40},{40,48},{48,56},{56,64},{64,7... | collective-permute-start | bytes 393224 | tf_op jit(solution)/shard_map/while/body/eval_jaxpr/ppermute | solution.py:19
  292.3 8.4 %collective-permute-start = (f32[2,128,128]{2,1,0:T(8,128)S(1)}, f32[2,128,128]{2,1,0:T(8,128)S(1)}, u32[]{:S(2)}, u32[]{:S(2)}) collective-permute-start(f32[2,128,128]{2,1,0:T(8,128)S(1)} %get-tuple-element.1212), channel_id=1, source_target_pairs={{0,8},{8,16},{16,24},{24,32},{32,40},{40,48},{48,56},{56,64},{64,7... | collective-permute-start | bytes 393224 | tf_op jit(solution)/shard_map/while/body/eval_jaxpr/ppermute | solution.py:19
  301.3 8.4 %collective-permute-start = (f32[2,128,128]{2,1,0:T(8,128)S(1)}, f32[2,128,128]{2,1,0:T(8,128)S(1)}, u32[]{:S(2)}, u32[]{:S(2)}) collective-permute-start(f32[2,128,128]{2,1,0:T(8,128)S(1)} %get-tuple-element.1212), channel_id=1, source_target_pairs={{0,8},{8,16},{16,24},{24,32},{32,40},{40,48},{48,56},{56,64},{64,7... | collective-permute-start | bytes 393224 | tf_op jit(solution)/shard_map/while/body/eval_jaxpr/ppermute | solution.py:19
  313.2 394.7 %reduce-scatter.7.cloned.1.call-start = ((), (), s32[]{:S(2)}) async-start(), calls=%async_computation.3 | async-start | bytes 2162688
  343.6 15.0 %collective-permute-start.1 = (f32[2,128,128]{2,1,0:T(8,128)S(1)}, f32[2,128,128]{2,1,0:T(8,128)S(1)}, u32[]{:S(2)}, u32[]{:S(2)}) collective-permute-start(f32[2,128,128]{2,1,0:T(8,128)S(1)} %get-tuple-element.1230), channel_id=1, source_target_pairs={{8,0},{16,8},{24,16},{32,24},{40,32},{48,40},{56,48},{64,56},{72,6... | collective-permute-start | bytes 393224 | tf_op jit(solution)/shard_map/while/body/eval_jaxpr/ppermute | solution.py:19
  359.3 8.4 %collective-permute-start.1 = (f32[2,128,128]{2,1,0:T(8,128)S(1)}, f32[2,128,128]{2,1,0:T(8,128)S(1)}, u32[]{:S(2)}, u32[]{:S(2)}) collective-permute-start(f32[2,128,128]{2,1,0:T(8,128)S(1)} %get-tuple-element.1230), channel_id=1, source_target_pairs={{8,0},{16,8},{24,16},{32,24},{40,32},{48,40},{56,48},{64,56},{72,6... | collective-permute-start | bytes 393224 | tf_op jit(solution)/shard_map/while/body/eval_jaxpr/ppermute | solution.py:19
  368.3 8.4 %collective-permute-start.1 = (f32[2,128,128]{2,1,0:T(8,128)S(1)}, f32[2,128,128]{2,1,0:T(8,128)S(1)}, u32[]{:S(2)}, u32[]{:S(2)}) collective-permute-start(f32[2,128,128]{2,1,0:T(8,128)S(1)} %get-tuple-element.1230), channel_id=1, source_target_pairs={{8,0},{16,8},{24,16},{32,24},{40,32},{48,40},{56,48},{64,56},{72,6... | collective-permute-start | bytes 393224 | tf_op jit(solution)/shard_map/while/body/eval_jaxpr/ppermute | solution.py:19
  377.4 8.4 %collective-permute-start.1 = (f32[2,128,128]{2,1,0:T(8,128)S(1)}, f32[2,128,128]{2,1,0:T(8,128)S(1)}, u32[]{:S(2)}, u32[]{:S(2)}) collective-permute-start(f32[2,128,128]{2,1,0:T(8,128)S(1)} %get-tuple-element.1230), channel_id=1, source_target_pairs={{8,0},{16,8},{24,16},{32,24},{40,32},{48,40},{56,48},{64,56},{72,6... | collective-permute-start | bytes 393224 | tf_op jit(solution)/shard_map/while/body/eval_jaxpr/ppermute | solution.py:19
  386.4 8.4 %collective-permute-start.1 = (f32[2,128,128]{2,1,0:T(8,128)S(1)}, f32[2,128,128]{2,1,0:T(8,128)S(1)}, u32[]{:S(2)}, u32[]{:S(2)}) collective-permute-start(f32[2,128,128]{2,1,0:T(8,128)S(1)} %get-tuple-element.1230), channel_id=1, source_target_pairs={{8,0},{16,8},{24,16},{32,24},{40,32},{48,40},{56,48},{64,56},{72,6... | collective-permute-start | bytes 393224 | tf_op jit(solution)/shard_map/while/body/eval_jaxpr/ppermute | solution.py:19
  395.5 8.4 %collective-permute-start.1 = (f32[2,128,128]{2,1,0:T(8,128)S(1)}, f32[2,128,128]{2,1,0:T(8,128)S(1)}, u32[]{:S(2)}, u32[]{:S(2)}) collective-permute-start(f32[2,128,128]{2,1,0:T(8,128)S(1)} %get-tuple-element.1230), channel_id=1, source_target_pairs={{8,0},{16,8},{24,16},{32,24},{40,32},{48,40},{56,48},{64,56},{72,6... | collective-permute-start | bytes 393224 | tf_op jit(solution)/shard_map/while/body/eval_jaxpr/ppermute | solution.py:19
  404.5 9.8 %collective-permute-start.1 = (f32[2,128,128]{2,1,0:T(8,128)S(1)}, f32[2,128,128]{2,1,0:T(8,128)S(1)}, u32[]{:S(2)}, u32[]{:S(2)}) collective-permute-start(f32[2,128,128]{2,1,0:T(8,128)S(1)} %get-tuple-element.1230), channel_id=1, source_target_pairs={{8,0},{16,8},{24,16},{32,24},{40,32},{48,40},{56,48},{64,56},{72,6... | collective-permute-start | bytes 393224 | tf_op jit(solution)/shard_map/while/body/eval_jaxpr/ppermute | solution.py:19
  415.0 8.6 %collective-permute-start.1 = (f32[2,128,128]{2,1,0:T(8,128)S(1)}, f32[2,128,128]{2,1,0:T(8,128)S(1)}, u32[]{:S(2)}, u32[]{:S(2)}) collective-permute-start(f32[2,128,128]{2,1,0:T(8,128)S(1)} %get-tuple-element.1230), channel_id=1, source_target_pairs={{8,0},{16,8},{24,16},{32,24},{40,32},{48,40},{56,48},{64,56},{72,6... | collective-permute-start | bytes 393224 | tf_op jit(solution)/shard_map/while/body/eval_jaxpr/ppermute | solution.py:19
  424.2 8.4 %collective-permute-start.1 = (f32[2,128,128]{2,1,0:T(8,128)S(1)}, f32[2,128,128]{2,1,0:T(8,128)S(1)}, u32[]{:S(2)}, u32[]{:S(2)}) collective-permute-start(f32[2,128,128]{2,1,0:T(8,128)S(1)} %get-tuple-element.1230), channel_id=1, source_target_pairs={{8,0},{16,8},{24,16},{32,24},{40,32},{48,40},{56,48},{64,56},{72,6... | collective-permute-start | bytes 393224 | tf_op jit(solution)/shard_map/while/body/eval_jaxpr/ppermute | solution.py:19
  433.2 8.6 %collective-permute-start.1 = (f32[2,128,128]{2,1,0:T(8,128)S(1)}, f32[2,128,128]{2,1,0:T(8,128)S(1)}, u32[]{:S(2)}, u32[]{:S(2)}) collective-permute-start(f32[2,128,128]{2,1,0:T(8,128)S(1)} %get-tuple-element.1230), channel_id=1, source_target_pairs={{8,0},{16,8},{24,16},{32,24},{40,32},{48,40},{56,48},{64,56},{72,6... | collective-permute-start | bytes 393224 | tf_op jit(solution)/shard_map/while/body/eval_jaxpr/ppermute | solution.py:19
  442.5 8.4 %collective-permute-start.1 = (f32[2,128,128]{2,1,0:T(8,128)S(1)}, f32[2,128,128]{2,1,0:T(8,128)S(1)}, u32[]{:S(2)}, u32[]{:S(2)}) collective-permute-start(f32[2,128,128]{2,1,0:T(8,128)S(1)} %get-tuple-element.1230), channel_id=1, source_target_pairs={{8,0},{16,8},{24,16},{32,24},{40,32},{48,40},{56,48},{64,56},{72,6... | collective-permute-start | bytes 393224 | tf_op jit(solution)/shard_map/while/body/eval_jaxpr/ppermute | solution.py:19
  451.6 8.4 %collective-permute-start.1 = (f32[2,128,128]{2,1,0:T(8,128)S(1)}, f32[2,128,128]{2,1,0:T(8,128)S(1)}, u32[]{:S(2)}, u32[]{:S(2)}) collective-permute-start(f32[2,128,128]{2,1,0:T(8,128)S(1)} %get-tuple-element.1230), channel_id=1, source_target_pairs={{8,0},{16,8},{24,16},{32,24},{40,32},{48,40},{56,48},{64,56},{72,6... | collective-permute-start | bytes 393224 | tf_op jit(solution)/shard_map/while/body/eval_jaxpr/ppermute | solution.py:19
  460.6 8.4 %collective-permute-start.1 = (f32[2,128,128]{2,1,0:T(8,128)S(1)}, f32[2,128,128]{2,1,0:T(8,128)S(1)}, u32[]{:S(2)}, u32[]{:S(2)}) collective-permute-start(f32[2,128,128]{2,1,0:T(8,128)S(1)} %get-tuple-element.1230), channel_id=1, source_target_pairs={{8,0},{16,8},{24,16},{32,24},{40,32},{48,40},{56,48},{64,56},{72,6... | collective-permute-start | bytes 393224 | tf_op jit(solution)/shard_map/while/body/eval_jaxpr/ppermute | solution.py:19
  469.6 8.4 %collective-permute-start.1 = (f32[2,128,128]{2,1,0:T(8,128)S(1)}, f32[2,128,128]{2,1,0:T(8,128)S(1)}, u32[]{:S(2)}, u32[]{:S(2)}) collective-permute-start(f32[2,128,128]{2,1,0:T(8,128)S(1)} %get-tuple-element.1230), channel_id=1, source_target_pairs={{8,0},{16,8},{24,16},{32,24},{40,32},{48,40},{56,48},{64,56},{72,6... | collective-permute-start | bytes 393224 | tf_op jit(solution)/shard_map/while/body/eval_jaxpr/ppermute | solution.py:19
  478.7 8.4 %collective-permute-start.1 = (f32[2,128,128]{2,1,0:T(8,128)S(1)}, f32[2,128,128]{2,1,0:T(8,128)S(1)}, u32[]{:S(2)}, u32[]{:S(2)}) collective-permute-start(f32[2,128,128]{2,1,0:T(8,128)S(1)} %get-tuple-element.1230), channel_id=1, source_target_pairs={{8,0},{16,8},{24,16},{32,24},{40,32},{48,40},{56,48},{64,56},{72,6... | collective-permute-start | bytes 393224 | tf_op jit(solution)/shard_map/while/body/eval_jaxpr/ppermute | solution.py:19
  487.7 8.4 %collective-permute-start.1 = (f32[2,128,128]{2,1,0:T(8,128)S(1)}, f32[2,128,128]{2,1,0:T(8,128)S(1)}, u32[]{:S(2)}, u32[]{:S(2)}) collective-permute-start(f32[2,128,128]{2,1,0:T(8,128)S(1)} %get-tuple-element.1230), channel_id=1, source_target_pairs={{8,0},{16,8},{24,16},{32,24},{40,32},{48,40},{56,48},{64,56},{72,6... | collective-permute-start | bytes 393224 | tf_op jit(solution)/shard_map/while/body/eval_jaxpr/ppermute | solution.py:19
  496.8 8.4 %collective-permute-start.1 = (f32[2,128,128]{2,1,0:T(8,128)S(1)}, f32[2,128,128]{2,1,0:T(8,128)S(1)}, u32[]{:S(2)}, u32[]{:S(2)}) collective-permute-start(f32[2,128,128]{2,1,0:T(8,128)S(1)} %get-tuple-element.1230), channel_id=1, source_target_pairs={{8,0},{16,8},{24,16},{32,24},{40,32},{48,40},{56,48},{64,56},{72,6... | collective-permute-start | bytes 393224 | tf_op jit(solution)/shard_map/while/body/eval_jaxpr/ppermute | solution.py:19
  505.8 8.4 %collective-permute-start.1 = (f32[2,128,128]{2,1,0:T(8,128)S(1)}, f32[2,128,128]{2,1,0:T(8,128)S(1)}, u32[]{:S(2)}, u32[]{:S(2)}) collective-permute-start(f32[2,128,128]{2,1,0:T(8,128)S(1)} %get-tuple-element.1230), channel_id=1, source_target_pairs={{8,0},{16,8},{24,16},{32,24},{40,32},{48,40},{56,48},{64,56},{72,6... | collective-permute-start | bytes 393224 | tf_op jit(solution)/shard_map/while/body/eval_jaxpr/ppermute | solution.py:19
  514.8 8.4 %collective-permute-start.1 = (f32[2,128,128]{2,1,0:T(8,128)S(1)}, f32[2,128,128]{2,1,0:T(8,128)S(1)}, u32[]{:S(2)}, u32[]{:S(2)}) collective-permute-start(f32[2,128,128]{2,1,0:T(8,128)S(1)} %get-tuple-element.1230), channel_id=1, source_target_pairs={{8,0},{16,8},{24,16},{32,24},{40,32},{48,40},{56,48},{64,56},{72,6... | collective-permute-start | bytes 393224 | tf_op jit(solution)/shard_map/while/body/eval_jaxpr/ppermute | solution.py:19
  523.9 8.4 %collective-permute-start.1 = (f32[2,128,128]{2,1,0:T(8,128)S(1)}, f32[2,128,128]{2,1,0:T(8,128)S(1)}, u32[]{:S(2)}, u32[]{:S(2)}) collective-permute-start(f32[2,128,128]{2,1,0:T(8,128)S(1)} %get-tuple-element.1230), channel_id=1, source_target_pairs={{8,0},{16,8},{24,16},{32,24},{40,32},{48,40},{56,48},{64,56},{72,6... | collective-permute-start | bytes 393224 | tf_op jit(solution)/shard_map/while/body/eval_jaxpr/ppermute | solution.py:19
  532.9 8.4 %collective-permute-start.1 = (f32[2,128,128]{2,1,0:T(8,128)S(1)}, f32[2,128,128]{2,1,0:T(8,128)S(1)}, u32[]{:S(2)}, u32[]{:S(2)}) collective-permute-start(f32[2,128,128]{2,1,0:T(8,128)S(1)} %get-tuple-element.1230), channel_id=1, source_target_pairs={{8,0},{16,8},{24,16},{32,24},{40,32},{48,40},{56,48},{64,56},{72,6... | collective-permute-start | bytes 393224 | tf_op jit(solution)/shard_map/while/body/eval_jaxpr/ppermute | solution.py:19
  542.0 8.4 %collective-permute-start.1 = (f32[2,128,128]{2,1,0:T(8,128)S(1)}, f32[2,128,128]{2,1,0:T(8,128)S(1)}, u32[]{:S(2)}, u32[]{:S(2)}) collective-permute-start(f32[2,128,128]{2,1,0:T(8,128)S(1)} %get-tuple-element.1230), channel_id=1, source_target_pairs={{8,0},{16,8},{24,16},{32,24},{40,32},{48,40},{56,48},{64,56},{72,6... | collective-permute-start | bytes 393224 | tf_op jit(solution)/shard_map/while/body/eval_jaxpr/ppermute | solution.py:19
  551.0 8.4 %collective-permute-start.1 = (f32[2,128,128]{2,1,0:T(8,128)S(1)}, f32[2,128,128]{2,1,0:T(8,128)S(1)}, u32[]{:S(2)}, u32[]{:S(2)}) collective-permute-start(f32[2,128,128]{2,1,0:T(8,128)S(1)} %get-tuple-element.1230), channel_id=1, source_target_pairs={{8,0},{16,8},{24,16},{32,24},{40,32},{48,40},{56,48},{64,56},{72,6... | collective-permute-start | bytes 393224 | tf_op jit(solution)/shard_map/while/body/eval_jaxpr/ppermute | solution.py:19
  560.0 8.4 %collective-permute-start.1 = (f32[2,128,128]{2,1,0:T(8,128)S(1)}, f32[2,128,128]{2,1,0:T(8,128)S(1)}, u32[]{:S(2)}, u32[]{:S(2)}) collective-permute-start(f32[2,128,128]{2,1,0:T(8,128)S(1)} %get-tuple-element.1230), channel_id=1, source_target_pairs={{8,0},{16,8},{24,16},{32,24},{40,32},{48,40},{56,48},{64,56},{72,6... | collective-permute-start | bytes 393224 | tf_op jit(solution)/shard_map/while/body/eval_jaxpr/ppermute | solution.py:19
  569.1 8.4 %collective-permute-start.1 = (f32[2,128,128]{2,1,0:T(8,128)S(1)}, f32[2,128,128]{2,1,0:T(8,128)S(1)}, u32[]{:S(2)}, u32[]{:S(2)}) collective-permute-start(f32[2,128,128]{2,1,0:T(8,128)S(1)} %get-tuple-element.1230), channel_id=1, source_target_pairs={{8,0},{16,8},{24,16},{32,24},{40,32},{48,40},{56,48},{64,56},{72,6... | collective-permute-start | bytes 393224 | tf_op jit(solution)/shard_map/while/body/eval_jaxpr/ppermute | solution.py:19
  578.1 8.4 %collective-permute-start.1 = (f32[2,128,128]{2,1,0:T(8,128)S(1)}, f32[2,128,128]{2,1,0:T(8,128)S(1)}, u32[]{:S(2)}, u32[]{:S(2)}) collective-permute-start(f32[2,128,128]{2,1,0:T(8,128)S(1)} %get-tuple-element.1230), channel_id=1, source_target_pairs={{8,0},{16,8},{24,16},{32,24},{40,32},{48,40},{56,48},{64,56},{72,6... | collective-permute-start | bytes 393224 | tf_op jit(solution)/shard_map/while/body/eval_jaxpr/ppermute | solution.py:19
  587.2 8.4 %collective-permute-start.1 = (f32[2,128,128]{2,1,0:T(8,128)S(1)}, f32[2,128,128]{2,1,0:T(8,128)S(1)}, u32[]{:S(2)}, u32[]{:S(2)}) collective-permute-start(f32[2,128,128]{2,1,0:T(8,128)S(1)} %get-tuple-element.1230), channel_id=1, source_target_pairs={{8,0},{16,8},{24,16},{32,24},{40,32},{48,40},{56,48},{64,56},{72,6... | collective-permute-start | bytes 393224 | tf_op jit(solution)/shard_map/while/body/eval_jaxpr/ppermute | solution.py:19
  596.2 8.4 %collective-permute-start.1 = (f32[2,128,128]{2,1,0:T(8,128)S(1)}, f32[2,128,128]{2,1,0:T(8,128)S(1)}, u32[]{:S(2)}, u32[]{:S(2)}) collective-permute-start(f32[2,128,128]{2,1,0:T(8,128)S(1)} %get-tuple-element.1230), channel_id=1, source_target_pairs={{8,0},{16,8},{24,16},{32,24},{40,32},{48,40},{56,48},{64,56},{72,6... | collective-permute-start | bytes 393224 | tf_op jit(solution)/shard_map/while/body/eval_jaxpr/ppermute | solution.py:19
  605.2 8.4 %collective-permute-start.1 = (f32[2,128,128]{2,1,0:T(8,128)S(1)}, f32[2,128,128]{2,1,0:T(8,128)S(1)}, u32[]{:S(2)}, u32[]{:S(2)}) collective-permute-start(f32[2,128,128]{2,1,0:T(8,128)S(1)} %get-tuple-element.1230), channel_id=1, source_target_pairs={{8,0},{16,8},{24,16},{32,24},{40,32},{48,40},{56,48},{64,56},{72,6... | collective-permute-start | bytes 393224 | tf_op jit(solution)/shard_map/while/body/eval_jaxpr/ppermute | solution.py:19
  614.3 8.4 %collective-permute-start.1 = (f32[2,128,128]{2,1,0:T(8,128)S(1)}, f32[2,128,128]{2,1,0:T(8,128)S(1)}, u32[]{:S(2)}, u32[]{:S(2)}) collective-permute-start(f32[2,128,128]{2,1,0:T(8,128)S(1)} %get-tuple-element.1230), channel_id=1, source_target_pairs={{8,0},{16,8},{24,16},{32,24},{40,32},{48,40},{56,48},{64,56},{72,6... | collective-permute-start | bytes 393224 | tf_op jit(solution)/shard_map/while/body/eval_jaxpr/ppermute | solution.py:19
  623.3 8.4 %collective-permute-start.1 = (f32[2,128,128]{2,1,0:T(8,128)S(1)}, f32[2,128,128]{2,1,0:T(8,128)S(1)}, u32[]{:S(2)}, u32[]{:S(2)}) collective-permute-start(f32[2,128,128]{2,1,0:T(8,128)S(1)} %get-tuple-element.1230), channel_id=1, source_target_pairs={{8,0},{16,8},{24,16},{32,24},{40,32},{48,40},{56,48},{64,56},{72,6... | collective-permute-start | bytes 393224 | tf_op jit(solution)/shard_map/while/body/eval_jaxpr/ppermute | solution.py:19
  (127 other events, 648.4 us)
Sparse Core Ops, SparseCore 0:
  313.3 37.3 reduce-scatter.4
  355.2 87.5 reduce-scatter.6
where the time goes:
time: 718 us; the launch traced here: 715 us
  waiting for transfers between devices  268 us (37%)
  starting transfers between devices  257 us (36%)
  matrix products  73.5 us (10%)
  local copies, waits for them, and re-layouts  46.5 us (6%)
  other arithmetic  25.8 us (4%)
  blocking collectives  23.8 us (3%)
  between operations  14.4 us (2%)
    ppermute x62, waiting for transfers between devices, shifted(): return lax.ppermute(value, axis, pairs)  268 us
    ppermute x62, starting transfers between devices, shifted(): return lax.ppermute(value, axis, pairs)  257 us
    all_gather x1, blocking collectives, per_device(): full_grad = lax.all_gather(grad_out, 'head', axis=0, tiled=True)  23.8 us
    while x240, local copies, waits for them, and re-layouts  21.3 us
  transfers between devices with their start and end apart: 64, of which 62 were waited for; matrix products, arithmetic and copies ran while one was open for 13% of the time, Pallas kernels for 0%

commit v1 on v0

v1 whole, which is shorter than its diff:
```python
import functools

import jax
import jax.numpy as jnp
from jax import lax
from jax.experimental import pallas as pl
from jax.experimental.pallas import tpu as pltpu
from jax.sharding import PartitionSpec as P

f32 = jnp.float32
bf16 = jnp.bfloat16
MESH = pl.DeviceIdType.MESH


def split(x):
    hi = x.astype(bf16)
    return hi, (x - hi.astype(f32)).astype(bf16)


def mm(a, b, ca=1, cb=0):
    if not isinstance(a, tuple):
        a = (a,) if a.dtype == bf16 else split(a)
    if not isinstance(b, tuple):
        b = (b,) if b.dtype == bf16 else split(b)
    left, right = [a[0]], [b[0]]
    if len(a) == 2:
        left.append(a[1])
        right.append(b[0])
    if len(b) == 2:
        left.append(a[0])
        right.append(b[1])
    left = jnp.concatenate(left, axis=ca) if len(left) > 1 else left[0]
    right = jnp.concatenate(right, axis=cb) if len(right) > 1 else right[0]
    return lax.dot_general(left, right, (((ca,), (cb,)), ((), ())), preferred_element_type=f32)


def rows(*parts):
    parts = [p if isinstance(p, tuple) else split(p) for p in parts]
    return tuple(jnp.concatenate([p[i] for p in parts], axis=0) for i in range(2))


def cols(*parts):
    parts = [p if isinstance(p, tuple) else split(p) for p in parts]
    return tuple(jnp.concatenate([p[i] for p in parts], axis=1) for i in range(2))


def rowsum(x):
    return jnp.sum(x, axis=1, keepdims=True)


def kernel(
    n_ctx, n_head,
    docs_ref, q_ref, k_ref, v_ref, rate_ref, decay_ref, w_ref, g_ref,
    out_ref, gq_ref, gk_ref, gv_ref, grate_ref, gdecay_ref, wg_ref,
    gfull, tl_own, tl_pair, a_own, a_pair, tall, tsend, lslice, aslice, lsend, asend,
    ret_out, ret_in, sg_pair, sg_fin, lpart, lrecv, wpart, wrecv, keep,
    g_ss, g_rs, p_ss, p_rs, t_ss, t_rs, l_ss, l_rs, a_ss, a_rs, r_ss, r_rs, o_ss, o_rs, w_ss, w_rs,
):
    n_chip = n_ctx // 2
    c = lax.axis_index("ctx")
    z = lax.axis_index("head")
    chip = lax.div(c, 2)
    core = lax.rem(c, 2)
    partner = c + 1 - 2 * core
    tok = q_ref.shape[0]
    dim = 128
    n_docs = docs_ref.shape[0] - 1
    slice_rows = dim // n_chip

    barrier = pltpu.get_barrier_semaphore()

    def greet_head(i, carry):
        pl.semaphore_signal(barrier, inc=1, device_id=(c, lax.rem(z + i, n_head)), device_id_type=MESH)
        return carry

    def greet_ctx(i, carry):
        pl.semaphore_signal(barrier, inc=1, device_id=(lax.rem(c + i, n_ctx), z), device_id_type=MESH)
        return carry

    lax.fori_loop(1, n_head, greet_head, 0)
    lax.fori_loop(1, n_ctx, greet_ctx, 0)

    def grad_copy(i):
        return pltpu.make_async_remote_copy(
            src_ref=g_ref, dst_ref=gfull.at[z], send_sem=g_ss.at[i], recv_sem=g_rs.at[i],
            device_id=(c, lax.rem(z + i, n_head)), device_id_type=MESH)

    def pair_copy(i, src, dst):
        return pltpu.make_async_remote_copy(
            src_ref=src, dst_ref=dst, send_sem=p_ss.at[i], recv_sem=p_rs.at[i],
            device_id=(partner, z), device_id_type=MESH)

    def peer(i):
        return lax.rem(chip + i, n_chip)

    def t_copy(i):
        return pltpu.make_async_remote_copy(
            src_ref=tsend, dst_ref=tall.at[chip], send_sem=t_ss.at[i], recv_sem=t_rs.at[i],
            device_id=(peer(i) * 2 + core, z), device_id_type=MESH)

    def l_copy(i):
        return pltpu.make_async_remote_copy(
            src_ref=lsend.at[peer(i)], dst_ref=lslice.at[chip], send_sem=l_ss.at[i], recv_sem=l_rs.at[i],
            device_id=(peer(i) * 2 + core, z), device_id_type=MESH)

    def a_copy(i):
        return pltpu.make_async_remote_copy(
            src_ref=asend.at[peer(i)], dst_ref=aslice.at[chip], send_sem=a_ss.at[i], recv_sem=a_rs.at[i],
            device_id=(peer(i) * 2 + core, z), device_id_type=MESH)

    def r_copy(i):
        return pltpu.make_async_remote_copy(
            src_ref=ret_out.at[peer(i)], dst_ref=ret_in.at[chip], send_sem=r_ss.at[i], recv_sem=r_rs.at[i],
            device_id=(peer(i) * 2 + core, z), device_id_type=MESH)

    def o_copy(i):
        to = lax.rem(z + i, n_head)
        return pltpu.make_async_remote_copy(
            src_ref=lpart.at[to], dst_ref=lrecv.at[z], send_sem=o_ss.at[i], recv_sem=o_rs.at[i],
            device_id=(c, to), device_id_type=MESH)

    def w_copy(i):
        to = lax.rem(c + i, n_ctx)
        return pltpu.make_async_remote_copy(
            src_ref=wpart.at[to], dst_ref=wrecv.at[c], send_sem=w_ss.at[i], recv_sem=w_rs.at[i],
            device_id=(to, z), device_id_type=MESH)

    def start_all(copy, n):
        def body(i, carry):
            copy(i).start()
            return carry
        lax.fori_loop(1, n, body, 0)

    def recv_all(copy, n):
        def body(i, carry):
            copy(i).wait_recv()
            return carry
        lax.fori_loop(1, n, body, 0)

    def sent_all(copy, n):
        def body(i, carry):
            copy(i).wait_send()
            return carry
        lax.fori_loop(1, n, body, 0)

    q = q_ref[...].astype(f32)
    k = k_ref[...].astype(f32)
    q_inv = 1.0 / jnp.sqrt(rowsum(q * q) + 1e-6)
    k_inv = 1.0 / jnp.sqrt(rowsum(k * k) + 1e-6)
    qn = q * q_inv
    kn = k * k_inv
    ks, qs = split(kn), split(qn)
    dots = mm(rows(ks, qs), ks, 1, 1)
    kk, qk = dots[:tok], dots[tok:]
    ii = lax.broadcasted_iota(jnp.int32, (tok, tok), 0)
    jj = lax.broadcasted_iota(jnp.int32, (tok, tok), 1)
    first = c * tok
    seg_i = jnp.zeros((tok, tok), f32)
    seg_j = jnp.zeros((tok, tok), f32)
    seg_all = jnp.zeros((1, 1), f32)
    for d in range(n_docs):
        at = docs_ref[d] - first
        seg_i = seg_i + jnp.where((ii >= at) & (at >= 0), 1.0, 0.0)
        seg_j = seg_j + jnp.where((jj >= at) & (at >= 0), 1.0, 0.0)
    seg_all = seg_i[tok - 1:, :]
    same = jnp.where(seg_i == seg_j, 1.0, 0.0)
    low = jnp.where(ii >= jj, same, 0.0)
    strict = jnp.where(ii > jj, same, 0.0)
    eye = jnp.where(ii == jj, 1.0, 0.0)
    at_start = jnp.where(seg_i[:, :1] == 0.0, 1.0, 0.0)
    at_end = jnp.where(seg_i[:, :1] == seg_all[:, :1], 1.0, 0.0)
    no_reset = jnp.where(seg_all[:, :1] == 0.0, 1.0, 0.0)

    upto = jnp.where(ii <= jj, 1.0, 0.0)
    cum_rows = lax.dot_general(decay_ref[...], upto, (((1,), (0,)), ((), ())),
                               precision=lax.Precision.HIGHEST, preferred_element_type=f32)

    def column(row):
        return rowsum(jnp.where(ii == jj, row, 0.0))

    info = []
    for h in range(2):
        cr = cum_rows[h:h + 1]
        cc = column(cr)
        b = column(rate_ref[h:h + 1, :])
        last = cr[:, tok - 1:]
        info.append(dict(
            b=b,
            ratio=jnp.exp(jnp.where(low > 0.0, cc - cr, 0.0)) * low,
            f=jnp.exp(cc) * at_start,
            e=jnp.exp(last - cc) * at_end,
            w=jnp.exp(last) * no_reset,
        ))

    pl.semaphore_wait(barrier, n_head + n_ctx - 2)
    start_all(grad_copy, n_head)
    gfull[z] = g_ref[...]

    def same_block(width):
        shift = width.bit_length() - 1
        return lax.shift_right_logical(ii, shift) == lax.shift_right_logical(jj, shift)

    for h in range(2):
        t = info[h]
        t["kr"] = kk * t["ratio"] * strict
        t["n"] = t["b"] * t["kr"]
    for h in range(2):
        t = info[h]
        x = jnp.where(same_block(16), -t["n"], 0.0)
        xs = split(x)
        x2 = mm(xs, xs)
        x2s = split(x2)
        x4 = mm(x2s, x2s)
        x4s = split(x4)
        x8s = split(mm(x4s, x4s))
        m = eye + x
        m = m + mm(m, x2s)
        m = m + mm(m, x4s)
        m = m + mm(m, x8s)
        t["m"] = m
    for width in (16, 32, 64):
        for h in range(2):
            t = info[h]
            off = jnp.where(same_block(2 * width) & ~same_block(width), t["n"], 0.0)
            ms = split(t["m"])
            t["m"] = t["m"] - mm(ms, mm(off, ms))
    v_all = v_ref[...].astype(f32)
    for h in range(2):
        t = info[h]
        v = v_all[:, h * dim:(h + 1) * dim]
        t["v"] = v
        t["ms"] = split(t["m"])
        uw = mm(t["ms"], cols(t["b"] * v, (t["b"] * t["f"]) * kn))
        uws = split(uw)
        t["u"], t["wks"] = uw[:, :dim], (uws[0][:, dim:], uws[1][:, dim:])
        ek = t["e"] * kn
        t["eks"] = split(ek)
        lt = mm(uws, t["eks"], 0, 0)
        tl_own[h, 0] = t["w"] * eye - lt[dim:]
        tl_own[h, 1] = lt[:dim]
        t["uws"] = uws

    tl_pair[core] = tl_own[core]
    tl_copy = pair_copy(0, tl_own.at[1 - core], tl_pair.at[core])
    tl_copy.start()
    for h in range(2):
        t = info[h]
        p = qk * t["ratio"]
        t["ps"] = split(p)
        ow = mm(t["ps"], t["uws"])
        t["o"] = ow[:, :dim]
        t["qt"] = t["f"] * qn - ow[:, dim:]
        t["qts"] = split(t["qt"])
    tl_copy.wait_recv()
    t1s = split(tl_pair[1, 0])
    t0s = split(tl_pair[0, 0])
    pair_t = mm(rows(t0s, tl_pair[0, 1]), t1s)
    tsend[...] = pair_t[:dim]
    tall[chip] = pair_t[:dim]
    pair_l = (pair_t[dim:] + tl_pair[1, 1]).reshape(n_chip, slice_rows, dim)
    lsend[...] = pair_l
    start_all(t_copy, n_chip)
    start_all(l_copy, n_chip)
    lslice[chip] = lsend[chip]

    recv_all(grad_copy, n_head)
    full_grad = gfull[...].reshape(tok, g_ref.shape[1])
    weight = w_ref[...]
    d_core = lax.dot_general(full_grad, weight, (((1,), (1,)), ((), ())), preferred_element_type=f32)
    for h in range(2):
        t = info[h]
        t["do"] = d_core[:, h * dim:(h + 1) * dim]
        t["dos"] = split(t["do"])
        a_own[h] = mm(t["dos"], t["qts"], 0, 0)
    a_pair[core] = a_own[core]
    ap_copy = pair_copy(1, a_own.at[1 - core], a_pair.at[core])
    ap_copy.start()
    for h in range(2):
        t = info[h]
        t["pd"] = mm(t["ps"], t["dos"], 0, 0)
    ap_copy.wait_recv()
    asend[...] = (mm(a_pair[1], t0s, 1, 1) + a_pair[0]).reshape(n_chip, slice_rows, dim)
    start_all(a_copy, n_chip)
    aslice[chip] = asend[chip]

    recv_all(t_copy, n_chip)
    recv_all(l_copy, n_chip)
    recv_all(a_copy, n_chip)
    state = jnp.zeros((slice_rows, dim), f32)
    adjoint = jnp.zeros((slice_rows, dim), f32)
    for i in range(n_chip):
        j = n_chip - 1 - i
        ret_out[i, 0] = state
        ret_out[j, 1] = adjoint
        if i < n_chip - 1:
            state = mm(state, tall[i]) + lslice[i]
            adjoint = mm(adjoint, tall[j], 1, 1) + aslice[j]
    start_all(r_copy, n_chip)
    ret_in[chip] = ret_out[chip]
    recv_all(r_copy, n_chip)
    state = ret_in[:, 0].reshape(dim, dim)
    adjoint = ret_in[:, 1].reshape(dim, dim)
    sg_pair[0, 0] = state
    sg_pair[1, 0] = mm(state, t0s) + tl_pair[0, 1]
    sg_pair[0, 1] = mm(adjoint, t1s, 1, 1) + a_pair[1]
    sg_pair[1, 1] = adjoint
    sg_fin[core] = sg_pair[core]
    sg_copy = pair_copy(2, sg_pair.at[1 - core], sg_fin.at[core])
    sg_copy.start()
    sg_copy.wait_recv()

    mixed = []
    for h in range(2):
        t = info[h]
        t["s"] = sg_fin[h, 0]
        t["g"] = sg_fin[h, 1]
        t["ss"], t["gs"] = split(t["s"]), split(t["g"])
        both = mm(rows(t["qts"], t["wks"]), t["ss"], 1, 1)
        mixed.append((t["o"] + both[:tok]).astype(bf16))
        t["p"] = t["u"] - both[tok:]
    mixed = jnp.concatenate(mixed, axis=1)
    partial = lax.dot_general(mixed, weight, (((1,), (0,)), ((), ())), preferred_element_type=f32)
    lpart[...] = partial.astype(bf16).reshape(lpart.shape)
    start_all(o_copy, n_head)
    wpartial = lax.dot_general(full_grad, mixed, (((0,), (0,)), ((), ())), preferred_element_type=f32)
    wpart[...] = wpartial.astype(bf16).reshape(wpart.shape)
    start_all(w_copy, n_ctx)
    lrecv[z] = lpart[z]
    wrecv[c] = wpart[c]

    dqk = jnp.zeros((tok, tok), f32)
    dkk = jnp.zeros((tok, tok), f32)
    dq = jnp.zeros((tok, dim), f32)
    dk = jnp.zeros((tok, dim), f32)
    before = jnp.where(ii < jj, 1.0, 0.0).astype(bf16)
    for h in range(2):
        t = info[h]
        b, f, e = t["b"], t["f"], t["e"]
        pps = split(t["p"])
        pg = mm(pps, t["gs"])
        dp = t["pd"] + mm(t["eks"], t["gs"], 1, 1)
        dr = mm(t["ms"], dp, 0, 0)
        both = rows(t["dos"], dr)
        dpn = mm(both, pps, 1, 1)
        dos_s = mm(both, t["ss"])
        d_o_s, d_r_s = dos_s[:tok], dos_s[tok:]
        xp = dpn[:tok] * t["ratio"]
        xr = -dpn[tok:] * t["kr"]
        xn = -dpn[tok:] * (b * t["ratio"] * strict)
        dqk = dqk + xp
        dkk = dkk + xn
        x = xp * qk + b * xr
        alpha = rowsum(qn * d_o_s)
        beta = rowsum(kn * d_r_s)
        db = rowsum(dr * t["v"]) - f * beta + rowsum(xr)
        gv_ref[:, h * dim:(h + 1) * dim] = b * dr
        grate_ref[h:h + 1, :] = jnp.sum(jnp.where(ii == jj, db, 0.0), axis=0, keepdims=True)
        fdf = f * (alpha - b * beta)
        ede = e * rowsum(kn * pg)
        y = mm(x, before)
        terms = jnp.where(ii >= jj, y + fdf, ede)
        wdw = t["w"] * jnp.sum(rowsum(t["s"] * t["g"]), axis=0, keepdims=True)
        gdecay_ref[h:h + 1, :] = jnp.sum(terms, axis=0, keepdims=True) + wdw
        dq = dq + f * d_o_s
        dk = dk + e * pg - (b * f) * d_r_s
    ds = rows(dqk, dkk)
    direct = mm(ds, ks)
    turned = mm(ds, rows(qs, ks), 0, 0)
    dq = dq + direct[:tok]
    dk = dk + direct[tok:] + turned
    gq_ref[...] = q_inv * (dq - qn * rowsum(qn * dq))
    gk_ref[...] = k_inv * (dk - kn * rowsum(kn * dk))

    recv_all(o_copy, n_head)
    out_ref[...] = jnp.sum(lrecv[...].astype(f32), axis=0)
    recv_all(w_copy, n_ctx)
    wg_ref[...] = jnp.sum(wrecv[...].astype(f32), axis=0)

    tl_copy.wait_send()
    ap_copy.wait_send()
    sg_copy.wait_send()
    sent_all(grad_copy, n_head)
    sent_all(t_copy, n_chip)
    sent_all(l_copy, n_chip)
    sent_all(a_copy, n_chip)
    sent_all(r_copy, n_chip)
    sent_all(o_copy, n_head)
    sent_all(w_copy, n_ctx)


def per_device(n_ctx, n_head, queries, key_vectors, value_rows, write_rate, log_decay, doc_offsets, out_weight, grad_out):
    n_chip = n_ctx // 2
    tok, dim = queries.shape
    width = grad_out.shape[1]
    share = grad_out.shape[0]
    sl = dim // n_chip
    wrows = width // n_ctx
    vmem = pl.BlockSpec(memory_space=pltpu.VMEM)
    dma = pltpu.SemaphoreType.DMA
    scratch = [
        pltpu.VMEM((n_head, share, width), bf16),
        pltpu.VMEM((2, 2, dim, dim), f32), pltpu.VMEM((2, 2, dim, dim), f32),
        pltpu.VMEM((2, dim, dim), f32), pltpu.VMEM((2, dim, dim), f32),
        pltpu.VMEM((n_chip, dim, dim), f32), pltpu.VMEM((dim, dim), f32),
        pltpu.VMEM((n_chip, sl, dim), f32), pltpu.VMEM((n_chip, sl, dim), f32),
        pltpu.VMEM((n_chip, sl, dim), f32), pltpu.VMEM((n_chip, sl, dim), f32),
        pltpu.VMEM((n_chip, 2, sl, dim), f32), pltpu.VMEM((n_chip, 2, sl, dim), f32),
        pltpu.VMEM((2, 2, dim, dim), f32), pltpu.VMEM((2, 2, dim, dim), f32),
        pltpu.VMEM((n_head, share, width), bf16), pltpu.VMEM((n_head, share, width), bf16),
        pltpu.VMEM((n_ctx, wrows, 2 * dim), bf16), pltpu.VMEM((n_ctx, wrows, 2 * dim), bf16),
        pltpu.VMEM((8, dim), f32),
        dma((n_head,)), dma((n_head,)), dma((3,)), dma((3,)),
        dma((n_chip,)), dma((n_chip,)), dma((n_chip,)), dma((n_chip,)),
        dma((n_chip,)), dma((n_chip,)), dma((n_chip,)), dma((n_chip,)),
        dma((n_head,)), dma((n_head,)), dma((n_ctx,)), dma((n_ctx,)),
    ]
    return pl.pallas_call(
        functools.partial(kernel, n_ctx, n_head),
        out_shape=(
            jax.ShapeDtypeStruct((share, width), f32),
            jax.ShapeDtypeStruct((tok, dim), f32),
            jax.ShapeDtypeStruct((tok, dim), f32),
            jax.ShapeDtypeStruct((tok, 2 * dim), f32),
            jax.ShapeDtypeStruct((2, tok), f32),
            jax.ShapeDtypeStruct((2, tok), f32),
            jax.ShapeDtypeStruct((wrows, 2 * dim), f32),
        ),
        in_specs=[pl.BlockSpec(memory_space=pltpu.SMEM)] + [vmem] * 7,
        out_specs=(vmem,) * 7,
        scratch_shapes=scratch,
        compiler_params=pltpu.CompilerParams(collective_id=0, has_side_effects=True,
                                             vmem_limit_bytes=48 * 1024 * 1024),
        name="layer",
    )(doc_offsets, queries, key_vectors, value_rows, write_rate, log_decay, out_weight, grad_out)


def solution(mesh):
    n_ctx, n_head = mesh.shape["ctx"], mesh.shape["head"]
    return jax.shard_map(
        functools.partial(per_device, n_ctx, n_head),
        mesh=mesh,
        in_specs=(
            P("ctx", "head"), P("ctx", "head"), P("ctx", "head"), P("head", "ctx"), P("head", "ctx"),
            P(), P("head", None), P(("ctx", "head"), None),
        ),
        out_specs=(
            P(("ctx", "head"), None), P("ctx", "head"), P("ctx", "head"), P("ctx", "head"),
            P("head", "ctx"), P("head", "ctx"), P("ctx", "head"),
        ),
        check_vma=False,
    )
```

time: 718 us -> 73.6 us (0.10)
  the two profiles are of different devices: /device:TPU:15 before, /device:TPU:1 now
where the time goes in v1:
time: 73.6 us; the launch traced here: 73.2 us
  Pallas kernels  61.8 us (84%)
  local copies, waits for them, and re-layouts  10.7 us (15%)
    pallas_call x1, Pallas kernels, per_device(): pl.pallas_call(functools.partial(kernel, n_ctx, n_head), out_shape=(jax.S...  61.8 us
    unnamed x23, local copies, waits for them, and re-layouts  10.7 us

profile of v1, /device:TPU:1, one launch (start us, length us, event | category | flops | bytes accessed | tf_op | source)
XLA Modules:
  0.0 73.2 jit_solution(8339134976000041541)
XLA Ops:
  0.6 0.0 copy-start
  0.6 1.2 %copy-done = bf16[256,2048]{1,0:T(8,128)(2,1)S(1)} copy-done((bf16[256,2048]{1,0:T(8,128)(2,1)S(1)}, bf16[256,2048]{1,0:T(8,128)(2,1)}, u32[]{:S(2)}) %copy-start) | copy-done | bytes 1048600
  1.9 0.0 copy-start.1
  1.9 0.8 %copy-done.1 = bf16[128,256]{1,0:T(8,128)(2,1)S(1)} copy-done((bf16[128,256]{1,0:T(8,128)(2,1)S(1)}, bf16[128,256]{1,0:T(8,128)(2,1)}, u32[]{:S(2)}) %copy-start.1) | copy-done | bytes 65560
  2.7 0.0 copy-start.2
  2.7 0.8 %copy-done.2 = bf16[16,2048]{1,0:T(8,128)(2,1)S(1)} copy-done((bf16[16,2048]{1,0:T(8,128)(2,1)S(1)}, bf16[16,2048]{1,0:T(8,128)(2,1)}, u32[]{:S(2)}) %copy-start.2) | copy-done | bytes 65560
  3.5 0.0 copy-start.3
  3.5 0.8 %copy-done.3 = bf16[128,128]{1,0:T(8,128)(2,1)S(1)} copy-done((bf16[128,128]{1,0:T(8,128)(2,1)S(1)}, bf16[128,128]{1,0:T(8,128)(2,1)}, u32[]{:S(2)}) %copy-start.3) | copy-done | bytes 32792
  4.3 0.0 copy-start.4
  4.3 0.8 %copy-done.4 = bf16[128,128]{1,0:T(8,128)(2,1)S(1)} copy-done((bf16[128,128]{1,0:T(8,128)(2,1)S(1)}, bf16[128,128]{1,0:T(8,128)(2,1)}, u32[]{:S(2)}) %copy-start.4) | copy-done | bytes 32792
  5.1 0.0 copy-start.5
  5.1 0.7 copy-done.5
  5.7 0.0 copy-start.6
  5.7 0.7 copy-done.6
  6.4 0.0 copy-start.7
  6.4 0.7 copy-done.7
  7.1 61.8 %layer.1 = (f32[16,2048]{1,0:T(8,128)S(1)}, f32[128,128]{1,0:T(8,128)S(1)}, f32[128,128]{1,0:T(8,128)S(1)}, f32[128,256]{1,0:T(8,128)S(1)}, f32[2,128]{1,0:T(2,1...) custom-call(s32[5]{0:T(128)S(1)} %copy-done.7, bf16[128,128]{1,0:T(8,128)(2,1)S(1)} %copy-done.3, ...), custom_call_target="tpu_custom_call" | custom-call | tf_op jit(solution)/shard_map/layer/pallas_call | solution.py:417
  68.9 0.7 copy.22
  69.5 0.6 copy.23
  70.2 0.6 copy.24
  70.8 0.7 copy.25
  71.5 0.6 copy.26
  72.0 0.6 copy.27
  72.6 0.6 copy.28
Async XLA Ops:
  0.6 1.2 %copy-start = (bf16[256,2048]{1,0:T(8,128)(2,1)S(1)}, bf16[256,2048]{1,0:T(8,128)(2,1)}, u32[]{:S(2)}) copy-start(bf16[256,2048]{1,0:T(8,128)(2,1)} %w_ref.1) | copy-start | bytes 3145732
  1.9 0.8 %copy-start.1 = (bf16[128,256]{1,0:T(8,128)(2,1)S(1)}, bf16[128,256]{1,0:T(8,128)(2,1)}, u32[]{:S(2)}) copy-start(bf16[128,256]{1,0:T(8,128)(2,1)} %v_ref.1) | copy-start | bytes 196612
  2.7 0.8 %copy-start.2 = (bf16[16,2048]{1,0:T(8,128)(2,1)S(1)}, bf16[16,2048]{1,0:T(8,128)(2,1)}, u32[]{:S(2)}) copy-start(bf16[16,2048]{1,0:T(8,128)(2,1)} %g_ref.1) | copy-start | bytes 196612
  3.5 0.8 %copy-start.3 = (bf16[128,128]{1,0:T(8,128)(2,1)S(1)}, bf16[128,128]{1,0:T(8,128)(2,1)}, u32[]{:S(2)}) copy-start(bf16[128,128]{1,0:T(8,128)(2,1)} %q_ref.1) | copy-start | bytes 98308
  4.3 0.8 %copy-start.4 = (bf16[128,128]{1,0:T(8,128)(2,1)S(1)}, bf16[128,128]{1,0:T(8,128)(2,1)}, u32[]{:S(2)}) copy-start(bf16[128,128]{1,0:T(8,128)(2,1)} %k_ref.1) | copy-start | bytes 98308
  5.1 0.7 copy-start.5
  5.7 0.7 copy-start.6
  6.4 0.7 copy-start.7

commit v2 on v1

--- a/solution.py
+++ b/solution.py
@@ -50,22 +50,37 @@
 
 def kernel(
     n_ctx, n_head,
-    docs_ref, q_ref, k_ref, v_ref, rate_ref, decay_ref, w_ref, g_ref,
+    docs_hbm, q_hbm, k_hbm, v_hbm, rate_hbm, decay_hbm, w_hbm, g_hbm,
     out_ref, gq_ref, gk_ref, gv_ref, grate_ref, gdecay_ref, wg_ref,
+    docs_ref, q_ref, k_ref, v_ref, rate_ref, decay_ref, w_ref,
     gfull, tl_own, tl_pair, a_own, a_pair, tall, tsend, lslice, aslice, lsend, asend,
-    ret_out, ret_in, sg_pair, sg_fin, lpart, lrecv, wpart, wrecv, keep,
-    g_ss, g_rs, p_ss, p_rs, t_ss, t_rs, l_ss, l_rs, a_ss, a_rs, r_ss, r_rs, o_ss, o_rs, w_ss, w_rs,
+    ret_out, ret_in, sg_pair, sg_fin, lpart, lrecv, wpart, wrecv,
+    i_s, g_ss, g_rs, p_ss, p_rs, t_ss, t_rs, l_ss, l_rs, a_ss, a_rs, r_ss, r_rs, o_ss, o_rs, w_ss, w_rs,
 ):
     n_chip = n_ctx // 2
+    side = 4 if n_chip == 16 else 1
     c = lax.axis_index("ctx")
     z = lax.axis_index("head")
     chip = lax.div(c, 2)
     core = lax.rem(c, 2)
     partner = c + 1 - 2 * core
+    row = lax.div(chip, side)
+    col = lax.rem(chip, side)
     tok = q_ref.shape[0]
     dim = 128
+    width = w_ref.shape[1]
     n_docs = docs_ref.shape[0] - 1
     slice_rows = dim // n_chip
+
+    loads = [
+        pltpu.make_async_copy(src, dst, i_s.at[i])
+        for i, (src, dst) in enumerate((
+            (g_hbm, gfull.at[z]), (q_hbm, q_ref), (k_hbm, k_ref), (docs_hbm, docs_ref),
+            (rate_hbm, rate_ref), (decay_hbm, decay_ref), (v_hbm, v_ref), (w_hbm, w_ref),
+        ))
+    ]
+    for load in loads:
+        load.start()
 
     barrier = pltpu.get_barrier_semaphore()
 
@@ -80,10 +95,16 @@
     lax.fori_loop(1, n_head, greet_head, 0)
     lax.fori_loop(1, n_ctx, greet_ctx, 0)
 
-    def grad_copy(i):
-        return pltpu.make_async_remote_copy(
-            src_ref=g_ref, dst_ref=gfull.at[z], send_sem=g_ss.at[i], recv_sem=g_rs.at[i],
-            device_id=(c, lax.rem(z + i, n_head)), device_id_type=MESH)
+    halves = (pl.ds(0, width // 2), pl.ds(width // 2, width // 2))
+
+    def grad_copy(block, shift, i, half=None):
+        ref = gfull.at[block] if half is None else gfull.at[block, :, halves[half]]
+        return pltpu.make_async_remote_copy(
+            src_ref=ref, dst_ref=ref, send_sem=g_ss.at[i], recv_sem=g_rs.at[block, half or 0],
+            device_id=(c, lax.rem(z + shift + n_head, n_head)), device_id_type=MESH)
+
+    def zed(shift):
+        return lax.rem(z + shift + n_head, n_head)
 
     def pair_copy(i, src, dst):
         return pltpu.make_async_remote_copy(
@@ -93,10 +114,53 @@
     def peer(i):
         return lax.rem(chip + i, n_chip)
 
-    def t_copy(i):
-        return pltpu.make_async_remote_copy(
-            src_ref=tsend, dst_ref=tall.at[chip], send_sem=t_ss.at[i], recv_sem=t_rs.at[i],
-            device_id=(peer(i) * 2 + core, z), device_id_type=MESH)
+    def chip_at(first_shift, second_shift):
+        to_col = lax.rem(col + (1 - core) * first_shift + core * second_shift, side)
+        to_row = lax.rem(row + core * first_shift + (1 - core) * second_shift, side)
+        return to_row * side + to_col
+
+    upper, lower = pl.ds(0, dim // 2), pl.ds(dim // 2, dim // 2)
+    t_sent = []
+
+    def t_start(block, first_shift, second_shift, half=None):
+        ref = tall.at[block] if half is None else tall.at[block, (upper, lower)[half]]
+        copy = pltpu.make_async_remote_copy(
+            src_ref=ref, dst_ref=ref,
+            send_sem=t_ss.at[len(t_sent)], recv_sem=t_rs.at[block, half or 0],
+            device_id=(chip_at(first_shift, second_shift) * 2 + core, z), device_id_type=MESH)
+        copy.start()
+        t_sent.append(copy)
+
+    def t_wait(block, half=None):
+        ref = tall.at[block] if half is None else tall.at[block, (upper, lower)[half]]
+        pltpu.make_async_remote_copy(
+            src_ref=ref, dst_ref=ref, send_sem=t_ss.at[0], recv_sem=t_rs.at[block, half or 0],
+            device_id=(partner, z), device_id_type=MESH).wait_recv()
+
+    def t_own():
+        for shift in (1, 3, 2):
+            t_start(chip, shift, 0)
+            if shift != 2:
+                t_start(chip, 0, shift)
+
+    def t_first(*shifts):
+        for shift in shifts:
+            block = chip_at(shift, 0)
+            t_wait(block)
+            t_start(block, 0, 1)
+            t_start(block, 0, 3)
+
+    def t_second(*shifts):
+        for shift in shifts:
+            for came, to, half in ((3, 1, 0), (1, 3, 1)):
+                block = chip_at(shift, came)
+                t_wait(block)
+                t_start(block, 0, to, half)
+
+    def t_last():
+        for shift in (0, 1, 3, 2):
+            for half in range(2):
+                t_wait(chip_at(shift, 2), half)
 
     def l_copy(i):
         return pltpu.make_async_remote_copy(
@@ -143,6 +207,8 @@
             return carry
         lax.fori_loop(1, n, body, 0)
 
+    for load in loads[1:6]:
+        load.wait()
     q = q_ref[...].astype(f32)
     k = k_ref[...].astype(f32)
     q_inv = 1.0 / jnp.sqrt(rowsum(q * q) + 1e-6)
@@ -193,11 +259,20 @@
         ))
 
     pl.semaphore_wait(barrier, n_head + n_ctx - 2)
-    start_all(grad_copy, n_head)
-    gfull[z] = g_ref[...]
-
-    def same_block(width):
-        shift = width.bit_length() - 1
+    loads[0].wait()
+    g_sent = []
+
+    def g_start(*args):
+        copy = grad_copy(*args)
+        copy.start()
+        g_sent.append(copy)
+
+    if n_head > 1:
+        for i, shift in enumerate((2, -2, 1, -1)):
+            g_start(z, shift, i)
+
+    def same_block(size):
+        shift = size.bit_length() - 1
         return lax.shift_right_logical(ii, shift) == lax.shift_right_logical(jj, shift)
 
     for h in range(2):
@@ -218,12 +293,19 @@
         m = m + mm(m, x4s)
         m = m + mm(m, x8s)
         t["m"] = m
-    for width in (16, 32, 64):
+    for size in (16, 32, 64):
         for h in range(2):
             t = info[h]
-            off = jnp.where(same_block(2 * width) & ~same_block(width), t["n"], 0.0)
+            off = jnp.where(same_block(2 * size) & ~same_block(size), t["n"], 0.0)
             ms = split(t["m"])
             t["m"] = t["m"] - mm(ms, mm(off, ms))
+    if n_head > 1:
+        for sign, half in ((1, 0), (-1, 1)):
+            block = zed(-2 * sign)
+            grad_copy(block, sign, 0).wait_recv()
+            g_start(block, sign, len(g_sent))
+            g_start(block, 2 * sign, len(g_sent), half)
+    loads[6].wait()
     v_all = v_ref[...].astype(f32)
     for h in range(2):
         t = info[h]
@@ -255,16 +337,21 @@
     t1s = split(tl_pair[1, 0])
     t0s = split(tl_pair[0, 0])
     pair_t = mm(rows(t0s, tl_pair[0, 1]), t1s)
-    tsend[...] = pair_t[:dim]
     tall[chip] = pair_t[:dim]
     pair_l = (pair_t[dim:] + tl_pair[1, 1]).reshape(n_chip, slice_rows, dim)
     lsend[...] = pair_l
-    start_all(t_copy, n_chip)
+    if side > 1:
+        t_own()
     start_all(l_copy, n_chip)
     lslice[chip] = lsend[chip]
 
-    recv_all(grad_copy, n_head)
-    full_grad = gfull[...].reshape(tok, g_ref.shape[1])
+    if n_head > 1:
+        for shift in (1, -1, 3, -3):
+            grad_copy(zed(shift), 1, 0).wait_recv()
+        for half in range(2):
+            grad_copy(zed(4), 1, 0, half).wait_recv()
+    loads[7].wait()
+    full_grad = gfull[...].reshape(tok, width)
     weight = w_ref[...]
     d_core = lax.dot_general(full_grad, weight, (((1,), (1,)), ((), ())), preferred_element_type=f32)
     for h in range(2):
@@ -275,6 +362,10 @@
     a_pair[core] = a_own[core]
     ap_copy = pair_copy(1, a_own.at[1 - core], a_pair.at[core])
     ap_copy.start()
+    if side > 1:
+        t_first(1, 3)
+        t_second(0)
+        t_first(2)
     for h in range(2):
         t = info[h]
         t["pd"] = mm(t["ps"], t["dos"], 0, 0)
@@ -283,7 +374,10 @@
     start_all(a_copy, n_chip)
     aslice[chip] = asend[chip]
 
-    recv_all(t_copy, n_chip)
+    if side > 1:
+        t_second(1, 3)
+        t_second(2)
+        t_last()
     recv_all(l_copy, n_chip)
     recv_all(a_copy, n_chip)
     state = jnp.zeros((slice_rows, dim), f32)
@@ -379,8 +473,8 @@
     tl_copy.wait_send()
     ap_copy.wait_send()
     sg_copy.wait_send()
-    sent_all(grad_copy, n_head)
-    sent_all(t_copy, n_chip)
+    for copy in g_sent + t_sent:
+        copy.wait_send()
     sent_all(l_copy, n_chip)
     sent_all(a_copy, n_chip)
     sent_all(r_copy, n_chip)
@@ -396,8 +490,12 @@
     sl = dim // n_chip
     wrows = width // n_ctx
     vmem = pl.BlockSpec(memory_space=pltpu.VMEM)
+    hbm = pl.BlockSpec(memory_space=pltpu.HBM)
     dma = pltpu.SemaphoreType.DMA
     scratch = [
+        pltpu.SMEM(doc_offsets.shape, jnp.int32),
+        pltpu.VMEM((tok, dim), bf16), pltpu.VMEM((tok, dim), bf16), pltpu.VMEM((tok, 2 * dim), bf16),
+        pltpu.VMEM((2, tok), f32), pltpu.VMEM((2, tok), f32), pltpu.VMEM((2 * dim, width), bf16),
         pltpu.VMEM((n_head, share, width), bf16),
         pltpu.VMEM((2, 2, dim, dim), f32), pltpu.VMEM((2, 2, dim, dim), f32),
         pltpu.VMEM((2, dim, dim), f32), pltpu.VMEM((2, dim, dim), f32),
@@ -408,30 +506,47 @@
         pltpu.VMEM((2, 2, dim, dim), f32), pltpu.VMEM((2, 2, dim, dim), f32),
         pltpu.VMEM((n_head, share, width), bf16), pltpu.VMEM((n_head, share, width), bf16),
         pltpu.VMEM((n_ctx, wrows, 2 * dim), bf16), pltpu.VMEM((n_ctx, wrows, 2 * dim), bf16),
-        pltpu.VMEM((8, dim), f32),
-        dma((n_head,)), dma((n_head,)), dma((3,)), dma((3,)),
-        dma((n_chip,)), dma((n_chip,)), dma((n_chip,)), dma((n_chip,)),
+        dma((8,)),
+        dma((8,)), dma((n_head, 2)), dma((3,)), dma((3,)),
+        dma((19,)), dma((n_chip, 2)), dma((n_chip,)), dma((n_chip,)),
         dma((n_chip,)), dma((n_chip,)), dma((n_chip,)), dma((n_chip,)),
         dma((n_head,)), dma((n_head,)), dma((n_ctx,)), dma((n_ctx,)),
     ]
-    return pl.pallas_call(
+    shapes = (
+        jax.ShapeDtypeStruct((share, width), f32),
+        jax.ShapeDtypeStruct((tok, dim), f32),
+        jax.ShapeDtypeStruct((tok, dim), f32),
+        jax.ShapeDtypeStruct((tok, 2 * dim), f32),
+        jax.ShapeDtypeStruct((2, tok), f32),
+        jax.ShapeDtypeStruct((2, tok), f32),
+        jax.ShapeDtypeStruct((wrows, 2 * dim), f32),
+    )
+    results = pl.pallas_call(
         functools.partial(kernel, n_ctx, n_head),
-        out_shape=(
-            jax.ShapeDtypeStruct((share, width), f32),
-            jax.ShapeDtypeStruct((tok, dim), f32),
-            jax.ShapeDtypeStruct((tok, dim), f32),
-            jax.ShapeDtypeStruct((tok, 2 * dim), f32),
-            jax.ShapeDtypeStruct((2, tok), f32),
-            jax.ShapeDtypeStruct((2, tok), f32),
-            jax.ShapeDtypeStruct((wrows, 2 * dim), f32),
-        ),
-        in_specs=[pl.BlockSpec(memory_space=pltpu.SMEM)] + [vmem] * 7,
+        out_shape=shapes,
+        in_specs=[hbm] * 8,
         out_specs=(vmem,) * 7,
         scratch_shapes=scratch,
         compiler_params=pltpu.CompilerParams(collective_id=0, has_side_effects=True,
-                                             vmem_limit_bytes=48 * 1024 * 1024),
+                                             vmem_limit_bytes=60 * 1024 * 1024),
         name="layer",
     )(doc_offsets, queries, key_vectors, value_rows, write_rate, log_decay, out_weight, grad_out)
+    return pl.pallas_call(
+        emit,
+        out_shape=shapes,
+        in_specs=[vmem] * 7,
+        out_specs=(hbm,) * 7,
+        scratch_shapes=[dma((7,))],
+        name="emit",
+    )(*results)
+
+
+def emit(*refs):
+    copies = [pltpu.make_async_copy(refs[i], refs[7 + i], refs[14].at[i]) for i in range(7)]
+    for copy in copies:
+        copy.start()
+    for copy in copies:
+        copy.wait()
 
 
 def solution(mesh):

time: 73.6 us -> 66.3 us (0.901)
  local copies, waits for them, and re-layouts: 10.7 us -> 0 us
  Pallas kernels: 61.8 us -> 65.6 us
    unnamed x23 -> x0, local copies, waits for them, and re-layouts: 10.7 us -> none
    pallas_call x1 -> x2, Pallas kernels: 61.8 us -> 65.6 us  [the longest x1 63.7 us: per_device(): pl.pallas_call(functools.partial(kernel, n_ctx, n_head), out_shape=shapes...]
where the time goes in v2:
time: 66.3 us; the launch traced here: 66.2 us
  Pallas kernels  65.6 us (99%)
    pallas_call x1, Pallas kernels, per_device(): pl.pallas_call(functools.partial(kernel, n_ctx, n_head), out_shape=shapes...  63.7 us
    pallas_call x1, Pallas kernels, per_device(): pl.pallas_call(emit, out_shape=shapes, in_specs=[vmem] * 7, out_specs=(hb...  1.87 us

profile of v2, /device:TPU:1, one launch (start us, length us, event | category | flops | bytes accessed | tf_op | source)
XLA Modules:
  0.0 66.2 jit_solution(17484988465320493396)
XLA Ops:
  0.6 63.7 %layer.1 = (f32[16,2048]{1,0:T(8,128)}, f32[128,128]{1,0:T(8,128)}, f32[128,128]{1,0:T(8,128)}, f32[128,256]{1,0:T(8,128)}, f32[2,128]{1,0:T(2,128)}, /*index=5*/f32[2,128]{1,0:T(2,128)}, f32[64,256]{1,0:T(8,128)}) custom-call(s32[5]{0:T(128)} %docs_hbm.1, bf16[128,128]{1,0:T(8,128)(2,1)} %q_hbm.1, bf16[128,128]{1,0:T(8,128)(2,1)} %k_hbm.1, ...), custom_call_target="tpu_custom_call" | custom-call | tf_op jit(solution)/shard_map/layer/pallas_call | solution.py:524
  64.3 1.9 %emit.1 = (f32[16,2048]{1,0:T(8,128)}, f32[128,128]{1,0:T(8,128)}, f32[128,128]{1,0:T(8,128)}, f32[128,256]{1,0:T(8,128)}, f32[2,128]{1,0:T(2,128)}, /*index=5*/f32[2,128]{1,0:T(2,128)}, f32[64,256]{1,0:T(8,128)}) custom-call(f32[16,2048]{1,0:T(8,128)} %get-tuple-element.14.refs_0_, f32[128,128]{1,0:T(8,128)} %get-tuple-element.15.refs_1_, ...), custom_call_target="tpu_custom_call" | custom-call | tf_op jit(solution)/shard_map/emit/pallas_call | solution.py:534

commit v3 on v2

--- a/solution.py
+++ b/solution.py
@@ -53,9 +53,10 @@
     docs_hbm, q_hbm, k_hbm, v_hbm, rate_hbm, decay_hbm, w_hbm, g_hbm,
     out_ref, gq_ref, gk_ref, gv_ref, grate_ref, gdecay_ref, wg_ref,
     docs_ref, q_ref, k_ref, v_ref, rate_ref, decay_ref, w_ref,
-    gfull, tl_own, tl_pair, a_own, a_pair, tall, tsend, lslice, aslice, lsend, asend,
-    ret_out, ret_in, sg_pair, sg_fin, lpart, lrecv, wpart, wrecv,
-    i_s, g_ss, g_rs, p_ss, p_rs, t_ss, t_rs, l_ss, l_rs, a_ss, a_rs, r_ss, r_rs, o_ss, o_rs, w_ss, w_rs,
+    gfull, gcol, gturn, tl_own, tl_oth, a_own, a_oth, tall, mall, lslice, aslice, lsend, asend,
+    sret_out, sret_in, aret_out, aret_in, lpart, lrecv, wx_own, wx_oth,
+    i_s, g_ss, g_rs, e_ss, e_rs, h_ss, h_rs, p_ss, p_rs, t_ss, t_rs, m_ss, m_rs,
+    l_ss, l_rs, a_ss, a_rs, s_ss, s_rs, r_ss, r_rs, o_ss, o_rs,
 ):
     n_chip = n_ctx // 2
     side = 4 if n_chip == 16 else 1
@@ -95,99 +96,142 @@
     lax.fori_loop(1, n_head, greet_head, 0)
     lax.fori_loop(1, n_ctx, greet_ctx, 0)
 
-    halves = (pl.ds(0, width // 2), pl.ds(width // 2, width // 2))
-
-    def grad_copy(block, shift, i, half=None):
-        ref = gfull.at[block] if half is None else gfull.at[block, :, halves[half]]
-        return pltpu.make_async_remote_copy(
-            src_ref=ref, dst_ref=ref, send_sem=g_ss.at[i], recv_sem=g_rs.at[block, half or 0],
-            device_id=(c, lax.rem(z + shift + n_head, n_head)), device_id_type=MESH)
-
     def zed(shift):
         return lax.rem(z + shift + n_head, n_head)
+
+    def peer(i):
+        return lax.rem(chip + i, n_chip)
+
+    def fence(body):
+        pl.when(c >= 0)(body)
+
+    def across_head(buf, ss, rs, part):
+        sends = [(0, 2, None), (0, -2, None), (0, 1, None), (0, -1, None),
+                 (-2, 1, None), (-2, 2, 0), (2, -1, None), (2, -2, 1)]
+
+        def copy(i, block, shift, half):
+            ref = buf.at[block] if half is None else part(buf, block, half)
+            return pltpu.make_async_remote_copy(
+                src_ref=ref, dst_ref=ref, send_sem=ss.at[i], recv_sem=rs.at[block, half or 0],
+                device_id=(c, zed(shift)), device_id_type=MESH)
+
+        def start(*which):
+            for i in which:
+                origin, shift, half = sends[i]
+                copy(i, zed(origin), shift, half).start()
+
+        def received(*origins):
+            for origin in origins:
+                for half in ((0, 1) if origin == 4 else (None,)):
+                    copy(0, zed(origin), 1, half).wait_recv()
+
+        def relay():
+            received(-2)
+            start(4, 5)
+            received(2)
+            start(6, 7)
+
+        def sent():
+            for i, (origin, shift, half) in enumerate(sends):
+                copy(i, zed(origin), shift, half).wait_send()
+
+        return start, relay, received, sent
+
+    def chip_at(first_shift, second_shift):
+        to_col = lax.rem(col + (1 - core) * first_shift + core * second_shift, side)
+        to_row = lax.rem(row + core * first_shift + (1 - core) * second_shift, side)
+        return to_row * side + to_col
+
+    def across_plane(buf, ss, rs):
+        rows_of = buf.shape[1] // 2
+        sends = []
+
+        def copy(i, origin, to, half):
+            block = chip_at(*origin)
+            ref = buf.at[block] if half is None else buf.at[block, pl.ds(half * rows_of, rows_of)]
+            return pltpu.make_async_remote_copy(
+                src_ref=ref, dst_ref=ref, send_sem=ss.at[i], recv_sem=rs.at[block, half or 0],
+                device_id=(chip_at(*to) * 2 + core, z), device_id_type=MESH)
+
+        def start(origin, to, half=None):
+            sends.append((origin, to, half))
+            copy(len(sends) - 1, origin, to, half).start()
+
+        def received(origin, half=None):
+            copy(0, origin, (0, 1), half).wait_recv()
+
+        def own():
+            for shift in (1, 3, 2):
+                start((0, 0), (shift, 0))
+                if shift != 2:
+                    start((0, 0), (0, shift))
+
+        def first(*shifts):
+            for shift in shifts:
+                received((shift, 0))
+                start((shift, 0), (0, 1))
+                start((shift, 0), (0, 3))
+
+        def second(*shifts):
+            for shift in shifts:
+                for came, to, half in ((3, 1, 0), (1, 3, 1)):
+                    received((shift, came))
+                    start((shift, came), (0, to), half)
+
+        def last():
+            for shift in (0, 1, 3, 2):
+                for half in range(2):
+                    received((shift, 2), half)
+
+        def sent():
+            for i, args in enumerate(sends):
+                copy(i, *args).wait_send()
+
+        return own, first, second, last, sent
+
+    g_start, g_relay, g_received, g_sent = across_head(
+        gfull, g_ss, g_rs, lambda buf, block, half: buf.at[block, :, pl.ds(half * (width // 2), width // 2)])
+    h_start, h_relay, h_received, h_sent = across_head(
+        gcol, h_ss, h_rs, lambda buf, block, half: (
+            buf.at[block, pl.ds(half * (n_chip // 2), n_chip // 2)] if n_chip > 1
+            else buf.at[block, :, :, pl.ds(half * 128, 128)]))
+    t_own, t_first, t_second, t_last, t_sent = across_plane(tall, t_ss, t_rs)
+    m_own, m_first, m_second, m_last, m_sent = across_plane(mall, m_ss, m_rs)
 
     def pair_copy(i, src, dst):
         return pltpu.make_async_remote_copy(
             src_ref=src, dst_ref=dst, send_sem=p_ss.at[i], recv_sem=p_rs.at[i],
             device_id=(partner, z), device_id_type=MESH)
 
-    def peer(i):
-        return lax.rem(chip + i, n_chip)
-
-    def chip_at(first_shift, second_shift):
-        to_col = lax.rem(col + (1 - core) * first_shift + core * second_shift, side)
-        to_row = lax.rem(row + core * first_shift + (1 - core) * second_shift, side)
-        return to_row * side + to_col
-
-    upper, lower = pl.ds(0, dim // 2), pl.ds(dim // 2, dim // 2)
-    t_sent = []
-
-    def t_start(block, first_shift, second_shift, half=None):
-        ref = tall.at[block] if half is None else tall.at[block, (upper, lower)[half]]
-        copy = pltpu.make_async_remote_copy(
-            src_ref=ref, dst_ref=ref,
-            send_sem=t_ss.at[len(t_sent)], recv_sem=t_rs.at[block, half or 0],
-            device_id=(chip_at(first_shift, second_shift) * 2 + core, z), device_id_type=MESH)
-        copy.start()
-        t_sent.append(copy)
-
-    def t_wait(block, half=None):
-        ref = tall.at[block] if half is None else tall.at[block, (upper, lower)[half]]
-        pltpu.make_async_remote_copy(
-            src_ref=ref, dst_ref=ref, send_sem=t_ss.at[0], recv_sem=t_rs.at[block, half or 0],
-            device_id=(partner, z), device_id_type=MESH).wait_recv()
-
-    def t_own():
-        for shift in (1, 3, 2):
-            t_start(chip, shift, 0)
-            if shift != 2:
-                t_start(chip, 0, shift)
-
-    def t_first(*shifts):
-        for shift in shifts:
-            block = chip_at(shift, 0)
-            t_wait(block)
-            t_start(block, 0, 1)
-            t_start(block, 0, 3)
-
-    def t_second(*shifts):
-        for shift in shifts:
-            for came, to, half in ((3, 1, 0), (1, 3, 1)):
-                block = chip_at(shift, came)
-                t_wait(block)
-                t_start(block, 0, to, half)
-
-    def t_last():
-        for shift in (0, 1, 3, 2):
-            for half in range(2):
-                t_wait(chip_at(shift, 2), half)
-
-    def l_copy(i):
-        return pltpu.make_async_remote_copy(
-            src_ref=lsend.at[peer(i)], dst_ref=lslice.at[chip], send_sem=l_ss.at[i], recv_sem=l_rs.at[i],
-            device_id=(peer(i) * 2 + core, z), device_id_type=MESH)
-
-    def a_copy(i):
-        return pltpu.make_async_remote_copy(
-            src_ref=asend.at[peer(i)], dst_ref=aslice.at[chip], send_sem=a_ss.at[i], recv_sem=a_rs.at[i],
-            device_id=(peer(i) * 2 + core, z), device_id_type=MESH)
-
-    def r_copy(i):
-        return pltpu.make_async_remote_copy(
-            src_ref=ret_out.at[peer(i)], dst_ref=ret_in.at[chip], send_sem=r_ss.at[i], recv_sem=r_rs.at[i],
-            device_id=(peer(i) * 2 + core, z), device_id_type=MESH)
+    def to_chips(src_of, dst, ss, rs):
+        def copy(i):
+            return pltpu.make_async_remote_copy(
+                src_ref=src_of(peer(i)), dst_ref=dst, send_sem=ss.at[i], recv_sem=rs.at[i],
+                device_id=(peer(i) * 2 + core, z), device_id_type=MESH)
+        return copy
+
+    chip_width = width // n_chip
+    e_copy = to_chips(lambda to: gfull.at[z, :, pl.ds(pl.multiple_of(to * chip_width, 128), chip_width)],
+                      gcol.at[z, chip], e_ss, e_rs)
+    l_copy = to_chips(lambda to: lsend.at[to], lslice.at[chip], l_ss, l_rs)
+    a_copy = to_chips(lambda to: asend.at[to], aslice.at[chip], a_ss, a_rs)
+
+    def to_plane(src, dst, ss, rs):
+        def copy(i):
+            to = lax.rem(c + i, n_ctx)
+            return pltpu.make_async_remote_copy(
+                src_ref=src.at[lax.div(to, 2)], dst_ref=dst.at[core, chip],
+                send_sem=ss.at[i], recv_sem=rs.at[i], device_id=(to, z), device_id_type=MESH)
+        return copy
+
+    s_copy = to_plane(sret_out, sret_in, s_ss, s_rs)
+    r_copy = to_plane(aret_out, aret_in, r_ss, r_rs)
 
     def o_copy(i):
         to = lax.rem(z + i, n_head)
         return pltpu.make_async_remote_copy(
             src_ref=lpart.at[to], dst_ref=lrecv.at[z], send_sem=o_ss.at[i], recv_sem=o_rs.at[i],
             device_id=(c, to), device_id_type=MESH)
-
-    def w_copy(i):
-        to = lax.rem(c + i, n_ctx)
-        return pltpu.make_async_remote_copy(
-            src_ref=wpart.at[to], dst_ref=wrecv.at[c], send_sem=w_ss.at[i], recv_sem=w_rs.at[i],
-            device_id=(to, z), device_id_type=MESH)
 
     def start_all(copy, n):
         def body(i, carry):
@@ -260,16 +304,10 @@
 
     pl.semaphore_wait(barrier, n_head + n_ctx - 2)
     loads[0].wait()
-    g_sent = []
-
-    def g_start(*args):
-        copy = grad_copy(*args)
-        copy.start()
-        g_sent.append(copy)
-
     if n_head > 1:
-        for i, shift in enumerate((2, -2, 1, -1)):
-            g_start(z, shift, i)
+        fence(lambda: g_start(0, 1, 2, 3))
+    start_all(e_copy, n_chip)
+    gcol[z, chip] = gfull[z, :, pl.ds(pl.multiple_of(chip * chip_width, 128), chip_width)]
 
     def same_block(size):
         shift = size.bit_length() - 1
@@ -299,12 +337,6 @@
             off = jnp.where(same_block(2 * size) & ~same_block(size), t["n"], 0.0)
             ms = split(t["m"])
             t["m"] = t["m"] - mm(ms, mm(off, ms))
-    if n_head > 1:
-        for sign, half in ((1, 0), (-1, 1)):
-            block = zed(-2 * sign)
-            grad_copy(block, sign, 0).wait_recv()
-            g_start(block, sign, len(g_sent))
-            g_start(block, 2 * sign, len(g_sent), half)
     loads[6].wait()
     v_all = v_ref[...].astype(f32)
     for h in range(2):
@@ -322,34 +354,59 @@
         tl_own[h, 1] = lt[:dim]
         t["uws"] = uws
 
-    tl_pair[core] = tl_own[core]
-    tl_copy = pair_copy(0, tl_own.at[1 - core], tl_pair.at[core])
-    tl_copy.start()
+    tl_copy = pair_copy(0, tl_own, tl_oth)
+    fence(lambda: pair_copy(0, tl_own, tl_oth).start())
     for h in range(2):
         t = info[h]
         p = qk * t["ratio"]
+        t["p_mat"] = p
         t["ps"] = split(p)
         ow = mm(t["ps"], t["uws"])
         t["o"] = ow[:, :dim]
         t["qt"] = t["f"] * qn - ow[:, dim:]
         t["qts"] = split(t["qt"])
     tl_copy.wait_recv()
-    t1s = split(tl_pair[1, 0])
-    t0s = split(tl_pair[0, 0])
-    pair_t = mm(rows(t0s, tl_pair[0, 1]), t1s)
+    is_first = core == 0
+
+    def ordered(own, other):
+        return jnp.where(is_first, own, other), jnp.where(is_first, other, own)
+
+    t0, t1 = ordered(tl_own[core, 0], tl_oth[core, 0])
+    l0, l1 = ordered(tl_own[core, 1], tl_oth[core, 1])
+    pair_t = mm(rows(t0, l0), t1)
     tall[chip] = pair_t[:dim]
-    pair_l = (pair_t[dim:] + tl_pair[1, 1]).reshape(n_chip, slice_rows, dim)
-    lsend[...] = pair_l
+    lsend[...] = (pair_t[dim:] + l1).reshape(n_chip, slice_rows, dim)
     if side > 1:
-        t_own()
+        fence(t_own)
     start_all(l_copy, n_chip)
     lslice[chip] = lsend[chip]
-
     if n_head > 1:
-        for shift in (1, -1, 3, -3):
-            grad_copy(zed(shift), 1, 0).wait_recv()
-        for half in range(2):
-            grad_copy(zed(4), 1, 0, half).wait_recv()
+        fence(g_relay)
+    recv_all(e_copy, n_chip)
+    if n_head > 1:
+        fence(lambda: h_start(0, 1, 2, 3))
+
+    if side > 1:
+        @fence
+        def _():
+            t_first(1, 3)
+            t_second(0)
+            t_first(2)
+            t_second(1, 3)
+            t_second(2)
+            t_last()
+    recv_all(l_copy, n_chip)
+    state = jnp.zeros((slice_rows, dim), f32)
+    for i in range(n_chip):
+        sret_out[i] = state
+        if i < n_chip - 1:
+            state = mm(state, tall[i]) + lslice[i]
+    start_all(s_copy, n_ctx)
+    sret_in[core, chip] = sret_out[chip]
+
+    if n_head > 1:
+        g_received(1, -1, 3, -3, 4)
+        fence(h_relay)
     loads[7].wait()
     full_grad = gfull[...].reshape(tok, width)
     weight = w_ref[...]
@@ -359,68 +416,73 @@
         t["do"] = d_core[:, h * dim:(h + 1) * dim]
         t["dos"] = split(t["do"])
         a_own[h] = mm(t["dos"], t["qts"], 0, 0)
-    a_pair[core] = a_own[core]
-    ap_copy = pair_copy(1, a_own.at[1 - core], a_pair.at[core])
-    ap_copy.start()
-    if side > 1:
-        t_first(1, 3)
-        t_second(0)
-        t_first(2)
-    for h in range(2):
-        t = info[h]
-        t["pd"] = mm(t["ps"], t["dos"], 0, 0)
-    ap_copy.wait_recv()
-    asend[...] = (mm(a_pair[1], t0s, 1, 1) + a_pair[0]).reshape(n_chip, slice_rows, dim)
-    start_all(a_copy, n_chip)
-    aslice[chip] = asend[chip]
-
-    if side > 1:
-        t_second(1, 3)
-        t_second(2)
-        t_last()
-    recv_all(l_copy, n_chip)
-    recv_all(a_copy, n_chip)
-    state = jnp.zeros((slice_rows, dim), f32)
-    adjoint = jnp.zeros((slice_rows, dim), f32)
-    for i in range(n_chip):
-        j = n_chip - 1 - i
-        ret_out[i, 0] = state
-        ret_out[j, 1] = adjoint
-        if i < n_chip - 1:
-            state = mm(state, tall[i]) + lslice[i]
-            adjoint = mm(adjoint, tall[j], 1, 1) + aslice[j]
-    start_all(r_copy, n_chip)
-    ret_in[chip] = ret_out[chip]
-    recv_all(r_copy, n_chip)
-    state = ret_in[:, 0].reshape(dim, dim)
-    adjoint = ret_in[:, 1].reshape(dim, dim)
-    sg_pair[0, 0] = state
-    sg_pair[1, 0] = mm(state, t0s) + tl_pair[0, 1]
-    sg_pair[0, 1] = mm(adjoint, t1s, 1, 1) + a_pair[1]
-    sg_pair[1, 1] = adjoint
-    sg_fin[core] = sg_pair[core]
-    sg_copy = pair_copy(2, sg_pair.at[1 - core], sg_fin.at[core])
-    sg_copy.start()
-    sg_copy.wait_recv()
-
+    ap_copy = pair_copy(1, a_own, a_oth)
+    fence(lambda: pair_copy(1, a_own, a_oth).start())
+
+    recv_all(s_copy, n_ctx)
     mixed = []
     for h in range(2):
         t = info[h]
-        t["s"] = sg_fin[h, 0]
-        t["g"] = sg_fin[h, 1]
-        t["ss"], t["gs"] = split(t["s"]), split(t["g"])
+        state = sret_in[h].reshape(dim, dim)
+        t["s"] = jnp.where(is_first, state, mm(state, tl_oth[h, 0]) + tl_oth[h, 1])
+        t["ss"] = split(t["s"])
         both = mm(rows(t["qts"], t["wks"]), t["ss"], 1, 1)
         mixed.append((t["o"] + both[:tok]).astype(bf16))
         t["p"] = t["u"] - both[tok:]
     mixed = jnp.concatenate(mixed, axis=1)
+    mall[chip] = mixed
+    if side > 1:
+        fence(m_own)
     partial = lax.dot_general(mixed, weight, (((1,), (0,)), ((), ())), preferred_element_type=f32)
     lpart[...] = partial.astype(bf16).reshape(lpart.shape)
-    start_all(o_copy, n_head)
-    wpartial = lax.dot_general(full_grad, mixed, (((0,), (0,)), ((), ())), preferred_element_type=f32)
-    wpart[...] = wpartial.astype(bf16).reshape(wpart.shape)
-    start_all(w_copy, n_ctx)
+    if n_head > 1:
+        @fence
+        def _():
+            for i in (4, 3, 5, 2, 6, 1, 7):
+                o_copy(i).start()
     lrecv[z] = lpart[z]
-    wrecv[c] = wpart[c]
+
+    ap_copy.wait_recv()
+    a0, a1 = ordered(a_own[core], a_oth[core])
+    asend[...] = (mm(a1, t0, 1, 1) + a0).reshape(n_chip, slice_rows, dim)
+    start_all(a_copy, n_chip)
+    aslice[chip] = asend[chip]
+    if side > 1:
+        @fence
+        def _():
+            m_first(1, 3)
+            m_second(0)
+    for h in range(2):
+        t = info[h]
+        t["pps"] = split(t["p"])
+        t["pd"] = mm(t["ps"], t["dos"], 0, 0)
+        t["xp"] = mm(t["dos"], t["pps"], 1, 1) * t["ratio"]
+        t["d_o_s"] = mm(t["dos"], t["ss"])
+    recv_all(a_copy, n_chip)
+    adjoint = jnp.zeros((slice_rows, dim), f32)
+    for j in reversed(range(n_chip)):
+        aret_out[j] = adjoint
+        if j > 0:
+            adjoint = mm(adjoint, tall[j], 1, 1) + aslice[j]
+    start_all(r_copy, n_ctx)
+    aret_in[core, chip] = aret_out[chip]
+    if side > 1:
+        @fence
+        def _():
+            m_first(2)
+            m_second(1, 3)
+    if n_head > 1:
+        h_received(1, -1, 3, -3, 4)
+    for j in range(n_chip):
+        gturn[j] = gcol[:, j].reshape(tok, chip_width).T
+    if side > 1:
+        fence(lambda: m_second(2))
+    recv_all(r_copy, n_ctx)
+    for h in range(2):
+        t = info[h]
+        adjoint = aret_in[h].reshape(dim, dim)
+        t["g"] = jnp.where(is_first, mm(adjoint, tl_oth[h, 0], 1, 1) + a_oth[h], adjoint)
+        t["gs"] = split(t["g"])
 
     dqk = jnp.zeros((tok, tok), f32)
     dkk = jnp.zeros((tok, tok), f32)
@@ -430,17 +492,16 @@
     for h in range(2):
         t = info[h]
         b, f, e = t["b"], t["f"], t["e"]
-        pps = split(t["p"])
+        pps = t["pps"]
         pg = mm(pps, t["gs"])
         dp = t["pd"] + mm(t["eks"], t["gs"], 1, 1)
         dr = mm(t["ms"], dp, 0, 0)
-        both = rows(t["dos"], dr)
-        dpn = mm(both, pps, 1, 1)
-        dos_s = mm(both, t["ss"])
-        d_o_s, d_r_s = dos_s[:tok], dos_s[tok:]
-        xp = dpn[:tok] * t["ratio"]
-        xr = -dpn[tok:] * t["kr"]
-        xn = -dpn[tok:] * (b * t["ratio"] * strict)
+        drs = split(dr)
+        dn = -mm(drs, pps, 1, 1)
+        d_o_s, d_r_s = t["d_o_s"], mm(drs, t["ss"])
+        xp = t["xp"]
+        xr = dn * t["kr"]
+        xn = dn * (b * t["ratio"] * strict)
         dqk = dqk + xp
         dkk = dkk + xn
         x = xp * qk + b * xr
@@ -465,21 +526,35 @@
     gq_ref[...] = q_inv * (dq - qn * rowsum(qn * dq))
     gk_ref[...] = k_inv * (dk - kn * rowsum(kn * dk))
 
+    if side > 1:
+        m_last()
+    total = jnp.zeros((chip_width, 2 * dim), f32)
+    for j in range(n_chip):
+        total = total + lax.dot_general(gturn[j], mall[j], (((1,), (0,)), ((), ())), preferred_element_type=f32)
+    half = chip_width // 2
+    wx_own[0] = total[:half]
+    wx_own[1] = total[half:]
+    fence(lambda: pair_copy(2, wx_own.at[1 - core], wx_oth).start())
     recv_all(o_copy, n_head)
     out_ref[...] = jnp.sum(lrecv[...].astype(f32), axis=0)
-    recv_all(w_copy, n_ctx)
-    wg_ref[...] = jnp.sum(wrecv[...].astype(f32), axis=0)
+    wx_copy = pair_copy(2, wx_own.at[1 - core], wx_oth)
+    wx_copy.wait_recv()
+    wg_ref[...] = wx_own[core] + wx_oth[...]
 
     tl_copy.wait_send()
     ap_copy.wait_send()
-    sg_copy.wait_send()
-    for copy in g_sent + t_sent:
-        copy.wait_send()
+    wx_copy.wait_send()
+    if n_head > 1:
+        g_sent()
+        h_sent()
+    t_sent()
+    m_sent()
+    sent_all(e_copy, n_chip)
     sent_all(l_copy, n_chip)
     sent_all(a_copy, n_chip)
-    sent_all(r_copy, n_chip)
+    sent_all(s_copy, n_ctx)
+    sent_all(r_copy, n_ctx)
     sent_all(o_copy, n_head)
-    sent_all(w_copy, n_ctx)
 
 
 def per_device(n_ctx, n_head, queries, key_vectors, value_rows, write_rate, log_decay, doc_offsets, out_weight, grad_out):
@@ -497,20 +572,22 @@
         pltpu.VMEM((tok, dim), bf16), pltpu.VMEM((tok, dim), bf16), pltpu.VMEM((tok, 2 * dim), bf16),
         pltpu.VMEM((2, tok), f32), pltpu.VMEM((2, tok), f32), pltpu.VMEM((2 * dim, width), bf16),
         pltpu.VMEM((n_head, share, width), bf16),
+        pltpu.VMEM((n_head, n_chip, share, width // n_chip), bf16),
+        pltpu.VMEM((n_chip, width // n_chip, tok), bf16),
         pltpu.VMEM((2, 2, dim, dim), f32), pltpu.VMEM((2, 2, dim, dim), f32),
         pltpu.VMEM((2, dim, dim), f32), pltpu.VMEM((2, dim, dim), f32),
-        pltpu.VMEM((n_chip, dim, dim), f32), pltpu.VMEM((dim, dim), f32),
+        pltpu.VMEM((n_chip, dim, dim), f32), pltpu.VMEM((n_chip, tok, 2 * dim), bf16),
         pltpu.VMEM((n_chip, sl, dim), f32), pltpu.VMEM((n_chip, sl, dim), f32),
         pltpu.VMEM((n_chip, sl, dim), f32), pltpu.VMEM((n_chip, sl, dim), f32),
-        pltpu.VMEM((n_chip, 2, sl, dim), f32), pltpu.VMEM((n_chip, 2, sl, dim), f32),
-        pltpu.VMEM((2, 2, dim, dim), f32), pltpu.VMEM((2, 2, dim, dim), f32),
+        pltpu.VMEM((n_chip, sl, dim), f32), pltpu.VMEM((2, n_chip, sl, dim), f32),
+        pltpu.VMEM((n_chip, sl, dim), f32), pltpu.VMEM((2, n_chip, sl, dim), f32),
         pltpu.VMEM((n_head, share, width), bf16), pltpu.VMEM((n_head, share, width), bf16),
-        pltpu.VMEM((n_ctx, wrows, 2 * dim), bf16), pltpu.VMEM((n_ctx, wrows, 2 * dim), bf16),
+        pltpu.VMEM((2, wrows, 2 * dim), f32), pltpu.VMEM((wrows, 2 * dim), f32),
         dma((8,)),
-        dma((8,)), dma((n_head, 2)), dma((3,)), dma((3,)),
-        dma((19,)), dma((n_chip, 2)), dma((n_chip,)), dma((n_chip,)),
+        dma((8,)), dma((n_head, 2)), dma((n_chip,)), dma((n_chip,)), dma((8,)), dma((n_head, 2)), dma((3,)), dma((3,)),
+        dma((19,)), dma((n_chip, 2)), dma((19,)), dma((n_chip, 2)),
         dma((n_chip,)), dma((n_chip,)), dma((n_chip,)), dma((n_chip,)),
-        dma((n_head,)), dma((n_head,)), dma((n_ctx,)), dma((n_ctx,)),
+        dma((n_ctx,)), dma((n_ctx,)), dma((n_ctx,)), dma((n_ctx,)), dma((n_head,)), dma((n_head,)),
     ]
     shapes = (
         jax.ShapeDtypeStruct((share, width), f32),

time: 66.3 us -> 61.3 us (0.925)
  Pallas kernels: 65.6 us -> 60.6 us
    pallas_call x1, Pallas kernels: 63.7 us -> 58.7 us  [per_device(): pl.pallas_call(functools.partial(kernel, n_ctx, n_head), out_shape=shapes...]
where the time goes in v3:
time: 61.3 us; the launch traced here: 61.2 us
  Pallas kernels  60.6 us (99%)
  between operations  0.64 us (1%)
    pallas_call x1, Pallas kernels, per_device(): pl.pallas_call(functools.partial(kernel, n_ctx, n_head), out_shape=shapes...  58.7 us
    pallas_call x1, Pallas kernels, per_device(): pl.pallas_call(emit, out_shape=shapes, in_specs=[vmem] * 7, out_specs=(hb...  1.87 us

profile of v3, /device:TPU:1, one launch (start us, length us, event | category | flops | bytes accessed | tf_op | source)
XLA Modules:
  0.0 61.2 jit_solution(7039848885597578461)
XLA Ops:
  0.6 58.7 %layer.1 = (f32[16,2048]{1,0:T(8,128)}, f32[128,128]{1,0:T(8,128)}, f32[128,128]{1,0:T(8,128)}, f32[128,256]{1,0:T(8,128)}, f32[2,128]{1,0:T(2,128)}, /*index=5*/f32[2,128]{1,0:T(2,128)}, f32[64,256]{1,0:T(8,128)}) custom-call(s32[5]{0:T(128)} %docs_hbm.1, bf16[128,128]{1,0:T(8,128)(2,1)} %q_hbm.1, bf16[128,128]{1,0:T(8,128)(2,1)} %k_hbm.1, ...), custom_call_target="tpu_custom_call" | custom-call | tf_op jit(solution)/shard_map/layer/pallas_call | solution.py:601
  59.3 1.9 %emit.1 = (f32[16,2048]{1,0:T(8,128)}, f32[128,128]{1,0:T(8,128)}, f32[128,128]{1,0:T(8,128)}, f32[128,256]{1,0:T(8,128)}, f32[2,128]{1,0:T(2,128)}, /*index=5*/f32[2,128]{1,0:T(2,128)}, f32[64,256]{1,0:T(8,128)}) custom-call(f32[16,2048]{1,0:T(8,128)} %get-tuple-element.14.refs_0_, f32[128,128]{1,0:T(8,128)} %get-tuple-element.15.refs_1_, ...), custom_call_target="tpu_custom_call" | custom-call | tf_op jit(solution)/shard_map/emit/pallas_call | solution.py:611

commit v4 on v3

--- a/solution.py
+++ b/solution.py
@@ -54,7 +54,7 @@
     out_ref, gq_ref, gk_ref, gv_ref, grate_ref, gdecay_ref, wg_ref,
     docs_ref, q_ref, k_ref, v_ref, rate_ref, decay_ref, w_ref,
     gfull, gcol, gturn, tl_own, tl_oth, a_own, a_oth, tall, mall, lslice, aslice, lsend, asend,
-    sret_out, sret_in, aret_out, aret_in, lpart, lrecv, wx_own, wx_oth,
+    sret_out, sret_in, aret_out, aret_in, lpart, lfull, lsum, lrecv, wx_own, wx_oth,
     i_s, g_ss, g_rs, e_ss, e_rs, h_ss, h_rs, p_ss, p_rs, t_ss, t_rs, m_ss, m_rs,
     l_ss, l_rs, a_ss, a_rs, s_ss, s_rs, r_ss, r_rs, o_ss, o_rs,
 ):
@@ -228,10 +228,15 @@
     r_copy = to_plane(aret_out, aret_in, r_ss, r_rs)
 
     def o_copy(i):
-        to = lax.rem(z + i, n_head)
+        to, of, half = ((1, 1, None), (-1, -1, None), (1, 3, None), (-1, -3, None), (2, 4, 0), (-2, 4, 1),
+                        (2, 2, None), (-2, -2, None))[i]
+        src, dst = (lpart.at[zed(of)] if i < 6 else lsum.at[i - 6]), lrecv.at[i]
+        if half is not None:
+            part = pl.ds(half * (width // 2), width // 2)
+            src, dst = lpart.at[zed(of), :, part], lrecv.at[i, :, part]
         return pltpu.make_async_remote_copy(
-            src_ref=lpart.at[to], dst_ref=lrecv.at[z], send_sem=o_ss.at[i], recv_sem=o_rs.at[i],
-            device_id=(c, to), device_id_type=MESH)
+            src_ref=src, dst_ref=dst, send_sem=o_ss.at[i], recv_sem=o_rs.at[i],
+            device_id=(c, zed(to)), device_id_type=MESH)
 
     def start_all(copy, n):
         def body(i, carry):
@@ -302,13 +307,6 @@
             w=jnp.exp(last) * no_reset,
         ))
 
-    pl.semaphore_wait(barrier, n_head + n_ctx - 2)
-    loads[0].wait()
-    if n_head > 1:
-        fence(lambda: g_start(0, 1, 2, 3))
-    start_all(e_copy, n_chip)
-    gcol[z, chip] = gfull[z, :, pl.ds(pl.multiple_of(chip * chip_width, 128), chip_width)]
-
     def same_block(size):
         shift = size.bit_length() - 1
         return lax.shift_right_logical(ii, shift) == lax.shift_right_logical(jj, shift)
@@ -355,7 +353,14 @@
         t["uws"] = uws
 
     tl_copy = pair_copy(0, tl_own, tl_oth)
+    pl.semaphore_wait(barrier, n_head + n_ctx - 2)
     fence(lambda: pair_copy(0, tl_own, tl_oth).start())
+    loads[0].wait()
+    if n_head > 1:
+        fence(lambda: g_start(0, 1, 2, 3))
+    start_all(e_copy, n_chip)
+    gcol[z, chip] = gfull[z, :, pl.ds(pl.multiple_of(chip * chip_width, 128), chip_width)]
+
     for h in range(2):
         t = info[h]
         p = qk * t["ratio"]
@@ -380,11 +385,6 @@
         fence(t_own)
     start_all(l_copy, n_chip)
     lslice[chip] = lsend[chip]
-    if n_head > 1:
-        fence(g_relay)
-    recv_all(e_copy, n_chip)
-    if n_head > 1:
-        fence(lambda: h_start(0, 1, 2, 3))
 
     if side > 1:
         @fence
@@ -392,6 +392,14 @@
             t_first(1, 3)
             t_second(0)
             t_first(2)
+    if n_head > 1:
+        fence(g_relay)
+    recv_all(e_copy, n_chip)
+    if n_head > 1:
+        fence(lambda: h_start(0, 1, 2, 3))
+    if side > 1:
+        @fence
+        def _():
             t_second(1, 3)
             t_second(2)
             t_last()
@@ -406,7 +414,6 @@
 
     if n_head > 1:
         g_received(1, -1, 3, -3, 4)
-        fence(h_relay)
     loads[7].wait()
     full_grad = gfull[...].reshape(tok, width)
     weight = w_ref[...]
@@ -418,6 +425,17 @@
         a_own[h] = mm(t["dos"], t["qts"], 0, 0)
     ap_copy = pair_copy(1, a_own, a_oth)
     fence(lambda: pair_copy(1, a_own, a_oth).start())
+
+    for h in range(2):
+        t = info[h]
+        t["pd"] = mm(t["ps"], t["dos"], 0, 0)
+    ap_copy.wait_recv()
+    a0, a1 = ordered(a_own[core], a_oth[core])
+    asend[...] = (mm(a1, t0, 1, 1) + a0).reshape(n_chip, slice_rows, dim)
+    start_all(a_copy, n_chip)
+    aslice[chip] = asend[chip]
+    if n_head > 1:
+        fence(h_relay)
 
     recv_all(s_copy, n_ctx)
     mixed = []
@@ -434,19 +452,15 @@
     if side > 1:
         fence(m_own)
     partial = lax.dot_general(mixed, weight, (((1,), (0,)), ((), ())), preferred_element_type=f32)
-    lpart[...] = partial.astype(bf16).reshape(lpart.shape)
+    partial = partial.reshape(lpart.shape)
+    lpart[...] = partial.astype(bf16)
+    lfull[...] = partial
     if n_head > 1:
         @fence
         def _():
-            for i in (4, 3, 5, 2, 6, 1, 7):
+            for i in (4, 5, 2, 3, 0, 1):
                 o_copy(i).start()
-    lrecv[z] = lpart[z]
-
-    ap_copy.wait_recv()
-    a0, a1 = ordered(a_own[core], a_oth[core])
-    asend[...] = (mm(a1, t0, 1, 1) + a0).reshape(n_chip, slice_rows, dim)
-    start_all(a_copy, n_chip)
-    aslice[chip] = asend[chip]
+
     if side > 1:
         @fence
         def _():
@@ -455,7 +469,6 @@
     for h in range(2):
         t = info[h]
         t["pps"] = split(t["p"])
-        t["pd"] = mm(t["ps"], t["dos"], 0, 0)
         t["xp"] = mm(t["dos"], t["pps"], 1, 1) * t["ratio"]
         t["d_o_s"] = mm(t["dos"], t["ss"])
     recv_all(a_copy, n_chip)
@@ -466,6 +479,20 @@
             adjoint = mm(adjoint, tall[j], 1, 1) + aslice[j]
     start_all(r_copy, n_ctx)
     aret_in[core, chip] = aret_out[chip]
+    if n_head > 1:
+        for i in range(2, 6):
+            o_copy(i).wait_recv()
+        mid = width // 2
+        for i in range(2):
+            on = lfull[zed(2 - 4 * i)] + lrecv[2 + i].astype(f32)
+            more = lrecv[4 + i, :, i * mid:(i + 1) * mid].astype(f32)
+            lsum[i, :, i * mid:(i + 1) * mid] = (on[:, i * mid:(i + 1) * mid] + more).astype(bf16)
+            lsum[i, :, (1 - i) * mid:(2 - i) * mid] = on[:, (1 - i) * mid:(2 - i) * mid].astype(bf16)
+
+        @fence
+        def _():
+            o_copy(6).start()
+            o_copy(7).start()
     if side > 1:
         @fence
         def _():
@@ -535,8 +562,12 @@
     wx_own[0] = total[:half]
     wx_own[1] = total[half:]
     fence(lambda: pair_copy(2, wx_own.at[1 - core], wx_oth).start())
-    recv_all(o_copy, n_head)
-    out_ref[...] = jnp.sum(lrecv[...].astype(f32), axis=0)
+    result = lfull[z]
+    if n_head > 1:
+        for i in (0, 1, 6, 7):
+            o_copy(i).wait_recv()
+            result = result + lrecv[i].astype(f32)
+    out_ref[...] = result
     wx_copy = pair_copy(2, wx_own.at[1 - core], wx_oth)
     wx_copy.wait_recv()
     wg_ref[...] = wx_own[core] + wx_oth[...]
@@ -554,7 +585,9 @@
     sent_all(a_copy, n_chip)
     sent_all(s_copy, n_ctx)
     sent_all(r_copy, n_ctx)
-    sent_all(o_copy, n_head)
+    if n_head > 1:
+        for i in range(8):
+            o_copy(i).wait_send()
 
 
 def per_device(n_ctx, n_head, queries, key_vectors, value_rows, write_rate, log_decay, doc_offsets, out_weight, grad_out):
@@ -581,13 +614,14 @@
         pltpu.VMEM((n_chip, sl, dim), f32), pltpu.VMEM((n_chip, sl, dim), f32),
         pltpu.VMEM((n_chip, sl, dim), f32), pltpu.VMEM((2, n_chip, sl, dim), f32),
         pltpu.VMEM((n_chip, sl, dim), f32), pltpu.VMEM((2, n_chip, sl, dim), f32),
-        pltpu.VMEM((n_head, share, width), bf16), pltpu.VMEM((n_head, share, width), bf16),
+        pltpu.VMEM((n_head, share, width), bf16), pltpu.VMEM((n_head, share, width), f32),
+        pltpu.VMEM((2, share, width), bf16), pltpu.VMEM((8, share, width), bf16),
         pltpu.VMEM((2, wrows, 2 * dim), f32), pltpu.VMEM((wrows, 2 * dim), f32),
         dma((8,)),
         dma((8,)), dma((n_head, 2)), dma((n_chip,)), dma((n_chip,)), dma((8,)), dma((n_head, 2)), dma((3,)), dma((3,)),
         dma((19,)), dma((n_chip, 2)), dma((19,)), dma((n_chip, 2)),
         dma((n_chip,)), dma((n_chip,)), dma((n_chip,)), dma((n_chip,)),
-        dma((n_ctx,)), dma((n_ctx,)), dma((n_ctx,)), dma((n_ctx,)), dma((n_head,)), dma((n_head,)),
+        dma((n_ctx,)), dma((n_ctx,)), dma((n_ctx,)), dma((n_ctx,)), dma((8,)), dma((8,)),
     ]
     shapes = (
         jax.ShapeDtypeStruct((share, width), f32),

time: 61.3 us -> 56.7 us (0.925)
  Pallas kernels: 60.6 us -> 55.9 us
    pallas_call x1, Pallas kernels: 58.7 us -> 54 us  [per_device(): pl.pallas_call(functools.partial(kernel, n_ctx, n_head), out_shape=shapes...]
where the time goes in v4:
time: 56.7 us; the launch traced here: 56.6 us
  Pallas kernels  55.9 us (99%)
  between operations  0.64 us (1%)
    pallas_call x1, Pallas kernels, per_device(): pl.pallas_call(functools.partial(kernel, n_ctx, n_head), out_shape=shapes...  54 us
    pallas_call x1, Pallas kernels, per_device(): pl.pallas_call(emit, out_shape=shapes, in_specs=[vmem] * 7, out_specs=(hb...  1.87 us

profile of v4, /device:TPU:1, one launch (start us, length us, event | category | flops | bytes accessed | tf_op | source)
XLA Modules:
  0.0 56.6 jit_solution(12978140284928596423)
XLA Ops:
  0.6 54.0 %layer.1 = (f32[16,2048]{1,0:T(8,128)}, f32[128,128]{1,0:T(8,128)}, f32[128,128]{1,0:T(8,128)}, f32[128,256]{1,0:T(8,128)}, f32[2,128]{1,0:T(2,128)}, /*index=5*/f32[2,128]{1,0:T(2,128)}, f32[64,256]{1,0:T(8,128)}) custom-call(s32[5]{0:T(128)} %docs_hbm.1, bf16[128,128]{1,0:T(8,128)(2,1)} %q_hbm.1, bf16[128,128]{1,0:T(8,128)(2,1)} %k_hbm.1, ...), custom_call_target="tpu_custom_call" | custom-call | tf_op jit(solution)/shard_map/layer/pallas_call | solution.py:635
  54.7 1.9 %emit.1 = (f32[16,2048]{1,0:T(8,128)}, f32[128,128]{1,0:T(8,128)}, f32[128,128]{1,0:T(8,128)}, f32[128,256]{1,0:T(8,128)}, f32[2,128]{1,0:T(2,128)}, /*index=5*/f32[2,128]{1,0:T(2,128)}, f32[64,256]{1,0:T(8,128)}) custom-call(f32[16,2048]{1,0:T(8,128)} %get-tuple-element.14.refs_0_, f32[128,128]{1,0:T(8,128)} %get-tuple-element.15.refs_1_, ...), custom_call_target="tpu_custom_call" | custom-call | tf_op jit(solution)/shard_map/emit/pallas_call | solution.py:645

commit v5 on v4

--- a/solution.py
+++ b/solution.py
@@ -54,8 +54,8 @@
     out_ref, gq_ref, gk_ref, gv_ref, grate_ref, gdecay_ref, wg_ref,
     docs_ref, q_ref, k_ref, v_ref, rate_ref, decay_ref, w_ref,
     gfull, gcol, gturn, tl_own, tl_oth, a_own, a_oth, tall, mall, lslice, aslice, lsend, asend,
-    sret_out, sret_in, aret_out, aret_in, lpart, lfull, lsum, lrecv, wx_own, wx_oth,
-    i_s, g_ss, g_rs, e_ss, e_rs, h_ss, h_rs, p_ss, p_rs, t_ss, t_rs, m_ss, m_rs,
+    sret_out, sret_in, aret_out, aret_in, lpart, lfull, lsum, lrecv, wfull, wsend, wrecv,
+    i_s, g_ss, g_rs, e_ss, e_rs, h_ss, h_rs, p_ss, p_rs, t_ss, t_rs, m_ss, m_rs, n_ss, n_rs,
     l_ss, l_rs, a_ss, a_rs, s_ss, s_rs, r_ss, r_rs, o_ss, o_rs,
 ):
     n_chip = n_ctx // 2
@@ -193,10 +193,9 @@
         gfull, g_ss, g_rs, lambda buf, block, half: buf.at[block, :, pl.ds(half * (width // 2), width // 2)])
     h_start, h_relay, h_received, h_sent = across_head(
         gcol, h_ss, h_rs, lambda buf, block, half: (
-            buf.at[block, pl.ds(half * (n_chip // 2), n_chip // 2)] if n_chip > 1
-            else buf.at[block, :, :, pl.ds(half * 128, 128)]))
+            buf.at[block, pl.ds(half * (side // 2), side // 2)] if n_chip > 1
+            else buf.at[block, :, :, :, pl.ds(half * 128, 128)]))
     t_own, t_first, t_second, t_last, t_sent = across_plane(tall, t_ss, t_rs)
-    m_own, m_first, m_second, m_last, m_sent = across_plane(mall, m_ss, m_rs)
 
     def pair_copy(i, src, dst):
         return pltpu.make_async_remote_copy(
@@ -211,21 +210,41 @@
         return copy
 
     chip_width = width // n_chip
-    e_copy = to_chips(lambda to: gfull.at[z, :, pl.ds(pl.multiple_of(to * chip_width, 128), chip_width)],
-                      gcol.at[z, chip], e_ss, e_rs)
+    first_at = (1 - core) * col + core * row
+    second_at = (1 - core) * row + core * col
+
+    def columns(first, second):
+        of = (1 - core) * (second * side + first) + core * (first * side + second)
+        return pl.ds(pl.multiple_of(of * chip_width, 128), chip_width)
+
+    def e_copy(i):
+        shift, second = lax.div(i, side), lax.rem(i, side)
+        return pltpu.make_async_remote_copy(
+            src_ref=gfull.at[z, :, columns(lax.rem(first_at + shift, side), second)],
+            dst_ref=gcol.at[z, first_at, second], send_sem=e_ss.at[i], recv_sem=e_rs.at[i],
+            device_id=(chip_at(shift, 0) * 2 + core, z), device_id_type=MESH)
+
+    def m_copy(shift):
+        return pltpu.make_async_remote_copy(
+            src_ref=mall.at[first_at], dst_ref=mall.at[first_at], send_sem=m_ss.at[shift], recv_sem=m_rs.at[shift],
+            device_id=(chip_at(shift, 0) * 2 + core, z), device_id_type=MESH)
+
+    def n_copy(shift, to_core):
+        return pltpu.make_async_remote_copy(
+            src_ref=wsend.at[lax.rem(second_at + shift, side), to_core], dst_ref=wrecv.at[core, second_at],
+            send_sem=n_ss.at[shift, to_core], recv_sem=n_rs.at[core, second_at],
+            device_id=(chip_at(0, shift) * 2 + to_core, z), device_id_type=MESH)
+
+    def n_received(of_core, at):
+        pltpu.make_async_remote_copy(
+            src_ref=wsend.at[0, 0], dst_ref=wrecv.at[of_core, at], send_sem=n_ss.at[0, 0],
+            recv_sem=n_rs.at[of_core, at], device_id=(partner, z), device_id_type=MESH).wait_recv()
+
     l_copy = to_chips(lambda to: lsend.at[to], lslice.at[chip], l_ss, l_rs)
     a_copy = to_chips(lambda to: asend.at[to], aslice.at[chip], a_ss, a_rs)
 
-    def to_plane(src, dst, ss, rs):
-        def copy(i):
-            to = lax.rem(c + i, n_ctx)
-            return pltpu.make_async_remote_copy(
-                src_ref=src.at[lax.div(to, 2)], dst_ref=dst.at[core, chip],
-                send_sem=ss.at[i], recv_sem=rs.at[i], device_id=(to, z), device_id_type=MESH)
-        return copy
-
-    s_copy = to_plane(sret_out, sret_in, s_ss, s_rs)
-    r_copy = to_plane(aret_out, aret_in, r_ss, r_rs)
+    s_copy = to_chips(lambda to: sret_out.at[to], sret_in.at[core, chip], s_ss, s_rs)
+    r_copy = to_chips(lambda to: aret_out.at[to], aret_in.at[core, chip], r_ss, r_rs)
 
     def o_copy(i):
         to, of, half = ((1, 1, None), (-1, -1, None), (1, 3, None), (-1, -3, None), (2, 4, 0), (-2, 4, 1),
@@ -238,23 +257,23 @@
             src_ref=src, dst_ref=dst, send_sem=o_ss.at[i], recv_sem=o_rs.at[i],
             device_id=(c, zed(to)), device_id_type=MESH)
 
-    def start_all(copy, n):
+    def start_all(copy, n, low=1):
         def body(i, carry):
             copy(i).start()
             return carry
-        lax.fori_loop(1, n, body, 0)
-
-    def recv_all(copy, n):
+        lax.fori_loop(low, n, body, 0)
+
+    def recv_all(copy, n, low=1):
         def body(i, carry):
             copy(i).wait_recv()
             return carry
-        lax.fori_loop(1, n, body, 0)
-
-    def sent_all(copy, n):
+        lax.fori_loop(low, n, body, 0)
+
+    def sent_all(copy, n, low=1):
         def body(i, carry):
             copy(i).wait_send()
             return carry
-        lax.fori_loop(1, n, body, 0)
+        lax.fori_loop(low, n, body, 0)
 
     for load in loads[1:6]:
         load.wait()
@@ -358,8 +377,9 @@
     loads[0].wait()
     if n_head > 1:
         fence(lambda: g_start(0, 1, 2, 3))
-    start_all(e_copy, n_chip)
-    gcol[z, chip] = gfull[z, :, pl.ds(pl.multiple_of(chip * chip_width, 128), chip_width)]
+    start_all(e_copy, n_chip, side)
+    for second in range(side):
+        gcol[z, first_at, second] = gfull[z, :, columns(first_at, second)]
 
     for h in range(2):
         t = info[h]
@@ -386,6 +406,12 @@
     start_all(l_copy, n_chip)
     lslice[chip] = lsend[chip]
 
+    for h in range(2):
+        t = info[h]
+        through = mm(t["qts"], rows(tl_oth[h, 0], tl_oth[h, 1]), 1, 1)
+        t["qfs"] = split(jnp.where(is_first, t["qt"], through[:, :dim]))
+        t["of"] = t["o"] + jnp.where(is_first, 0.0, through[:, dim:])
+
     if side > 1:
         @fence
         def _():
@@ -394,7 +420,7 @@
             t_first(2)
     if n_head > 1:
         fence(g_relay)
-    recv_all(e_copy, n_chip)
+    recv_all(e_copy, n_chip, side)
     if n_head > 1:
         fence(lambda: h_start(0, 1, 2, 3))
     if side > 1:
@@ -409,7 +435,7 @@
         sret_out[i] = state
         if i < n_chip - 1:
             state = mm(state, tall[i]) + lslice[i]
-    start_all(s_copy, n_ctx)
+    start_all(s_copy, n_chip)
     sret_in[core, chip] = sret_out[chip]
 
     if n_head > 1:
@@ -437,48 +463,64 @@
     if n_head > 1:
         fence(h_relay)
 
-    recv_all(s_copy, n_ctx)
+    tl_copy.wait_send()
+    t_sent()
+    sent_all(e_copy, n_chip, side)
+    sent_all(l_copy, n_chip)
+    recv_all(s_copy, n_chip)
+    fence(lambda: pair_copy(2, sret_in.at[core], sret_in.at[core]).start())
+    pair_copy(2, sret_in.at[core], sret_in.at[1 - core]).wait_recv()
     mixed = []
     for h in range(2):
         t = info[h]
-        state = sret_in[h].reshape(dim, dim)
-        t["s"] = jnp.where(is_first, state, mm(state, tl_oth[h, 0]) + tl_oth[h, 1])
-        t["ss"] = split(t["s"])
-        both = mm(rows(t["qts"], t["wks"]), t["ss"], 1, 1)
-        mixed.append((t["o"] + both[:tok]).astype(bf16))
-        t["p"] = t["u"] - both[tok:]
+        t["ps_in"] = split(sret_in[h].reshape(dim, dim))
+        mixed.append((t["of"] + mm(t["qfs"], t["ps_in"], 1, 1)).astype(bf16))
     mixed = jnp.concatenate(mixed, axis=1)
-    mall[chip] = mixed
+    mall[first_at] = mixed
     if side > 1:
-        fence(m_own)
+        @fence
+        def _():
+            for shift in (2, 1, 3):
+                m_copy(shift).start()
     partial = lax.dot_general(mixed, weight, (((1,), (0,)), ((), ())), preferred_element_type=f32)
     partial = partial.reshape(lpart.shape)
     lpart[...] = partial.astype(bf16)
-    lfull[...] = partial
     if n_head > 1:
         @fence
         def _():
             for i in (4, 5, 2, 3, 0, 1):
                 o_copy(i).start()
-
-    if side > 1:
-        @fence
-        def _():
-            m_first(1, 3)
-            m_second(0)
-    for h in range(2):
-        t = info[h]
-        t["pps"] = split(t["p"])
-        t["xp"] = mm(t["dos"], t["pps"], 1, 1) * t["ratio"]
-        t["d_o_s"] = mm(t["dos"], t["ss"])
+    lfull[...] = partial
+
     recv_all(a_copy, n_chip)
     adjoint = jnp.zeros((slice_rows, dim), f32)
     for j in reversed(range(n_chip)):
         aret_out[j] = adjoint
         if j > 0:
             adjoint = mm(adjoint, tall[j], 1, 1) + aslice[j]
-    start_all(r_copy, n_ctx)
+    start_all(r_copy, n_chip)
     aret_in[core, chip] = aret_out[chip]
+    if n_head > 1:
+        h_received(1, -1, 3, -3, 4)
+    for second in range(side):
+        for first_of in range(side):
+            gturn[second * chip_width:(second + 1) * chip_width, first_of * tok:(first_of + 1) * tok] = (
+                gcol[:, first_of, second].reshape(tok, chip_width).T)
+    if side > 1:
+        for shift in (1, 3, 2):
+            m_copy(shift).wait_recv()
+    product = lax.dot_general(gturn[...], mall[...].reshape(side * tok, 2 * dim), (((1,), (0,)), ((), ())),
+                              preferred_element_type=f32).reshape(wfull.shape)
+    wsend[...] = product.astype(bf16)
+
+    @fence
+    def _():
+        for shift in (2, 1, 3)[:side - 1]:
+            for to_core in range(2):
+                n_copy(shift, to_core).start()
+        n_copy(0, 1 - core).start()
+    wfull[...] = product
+
     if n_head > 1:
         for i in range(2, 6):
             o_copy(i).wait_recv()
@@ -493,43 +535,54 @@
         def _():
             o_copy(6).start()
             o_copy(7).start()
-    if side > 1:
-        @fence
-        def _():
-            m_first(2)
-            m_second(1, 3)
-    if n_head > 1:
-        h_received(1, -1, 3, -3, 4)
-    for j in range(n_chip):
-        gturn[j] = gcol[:, j].reshape(tok, chip_width).T
-    if side > 1:
-        fence(lambda: m_second(2))
-    recv_all(r_copy, n_ctx)
+    dqk = jnp.zeros((tok, tok), f32)
+    dq = jnp.zeros((tok, dim), f32)
+    for h in range(2):
+        t = info[h]
+        state = sret_in[h].reshape(dim, dim)
+        t["s"] = jnp.where(is_first, state, mm(t["ps_in"], tl_oth[h, 0]) + tl_oth[h, 1])
+        t["ss"] = split(t["s"])
+        t["p"] = t["u"] - mm(t["wks"], t["ss"], 1, 1)
+        t["pps"] = split(t["p"])
+        t["xp"] = mm(t["dos"], t["pps"], 1, 1) * t["ratio"]
+        t["d_o_s"] = mm(t["dos"], t["ss"])
+        turned = mm(t["ms"], cols(t["pd"], t["eks"]), 0, 0)
+        t["dr0"], t["mes"] = turned[:, :dim], split(turned[:, dim:])
+        dqk = dqk + t["xp"]
+        dq = dq + t["f"] * t["d_o_s"]
+    dqks = split(dqk)
+    dq = dq + mm(dqks, ks)
+    dk = mm(dqks, qs, 0, 0)
+    gq_ref[...] = q_inv * (dq - qn * rowsum(qn * dq))
+    sent_all(s_copy, n_chip)
+    sent_all(a_copy, n_chip)
+    ap_copy.wait_send()
+    if n_head > 1:
+        g_sent()
+        h_sent()
+    recv_all(r_copy, n_chip)
+    fence(lambda: pair_copy(3, aret_in.at[core], aret_in.at[core]).start())
+    pair_copy(3, aret_in.at[core], aret_in.at[1 - core]).wait_recv()
     for h in range(2):
         t = info[h]
         adjoint = aret_in[h].reshape(dim, dim)
         t["g"] = jnp.where(is_first, mm(adjoint, tl_oth[h, 0], 1, 1) + a_oth[h], adjoint)
         t["gs"] = split(t["g"])
 
-    dqk = jnp.zeros((tok, tok), f32)
     dkk = jnp.zeros((tok, tok), f32)
-    dq = jnp.zeros((tok, dim), f32)
-    dk = jnp.zeros((tok, dim), f32)
     before = jnp.where(ii < jj, 1.0, 0.0).astype(bf16)
     for h in range(2):
         t = info[h]
         b, f, e = t["b"], t["f"], t["e"]
         pps = t["pps"]
         pg = mm(pps, t["gs"])
-        dp = t["pd"] + mm(t["eks"], t["gs"], 1, 1)
-        dr = mm(t["ms"], dp, 0, 0)
+        dr = t["dr0"] + mm(t["mes"], t["gs"], 1, 1)
         drs = split(dr)
         dn = -mm(drs, pps, 1, 1)
         d_o_s, d_r_s = t["d_o_s"], mm(drs, t["ss"])
         xp = t["xp"]
         xr = dn * t["kr"]
         xn = dn * (b * t["ratio"] * strict)
-        dqk = dqk + xp
         dkk = dkk + xn
         x = xp * qk + b * xr
         alpha = rowsum(qn * d_o_s)
@@ -543,48 +596,35 @@
         terms = jnp.where(ii >= jj, y + fdf, ede)
         wdw = t["w"] * jnp.sum(rowsum(t["s"] * t["g"]), axis=0, keepdims=True)
         gdecay_ref[h:h + 1, :] = jnp.sum(terms, axis=0, keepdims=True) + wdw
-        dq = dq + f * d_o_s
         dk = dk + e * pg - (b * f) * d_r_s
-    ds = rows(dqk, dkk)
-    direct = mm(ds, ks)
-    turned = mm(ds, rows(qs, ks), 0, 0)
-    dq = dq + direct[:tok]
-    dk = dk + direct[tok:] + turned
-    gq_ref[...] = q_inv * (dq - qn * rowsum(qn * dq))
+    ds = split(dkk)
+    dk = dk + mm(ds, ks) + mm(ds, ks, 0, 0)
     gk_ref[...] = k_inv * (dk - kn * rowsum(kn * dk))
 
-    if side > 1:
-        m_last()
-    total = jnp.zeros((chip_width, 2 * dim), f32)
-    for j in range(n_chip):
-        total = total + lax.dot_general(gturn[j], mall[j], (((1,), (0,)), ((), ())), preferred_element_type=f32)
-    half = chip_width // 2
-    wx_own[0] = total[:half]
-    wx_own[1] = total[half:]
-    fence(lambda: pair_copy(2, wx_own.at[1 - core], wx_oth).start())
     result = lfull[z]
     if n_head > 1:
         for i in (0, 1, 6, 7):
             o_copy(i).wait_recv()
             result = result + lrecv[i].astype(f32)
     out_ref[...] = result
-    wx_copy = pair_copy(2, wx_own.at[1 - core], wx_oth)
-    wx_copy.wait_recv()
-    wg_ref[...] = wx_own[core] + wx_oth[...]
-
-    tl_copy.wait_send()
-    ap_copy.wait_send()
-    wx_copy.wait_send()
-    if n_head > 1:
-        g_sent()
-        h_sent()
-    t_sent()
-    m_sent()
-    sent_all(e_copy, n_chip)
-    sent_all(l_copy, n_chip)
-    sent_all(a_copy, n_chip)
-    sent_all(s_copy, n_ctx)
-    sent_all(r_copy, n_ctx)
+    total = wfull[second_at, core]
+    for shift in range(1, side):
+        at = lax.rem(second_at + shift, side)
+        n_received(core, at)
+        total = total + wrecv[core, at].astype(f32)
+    for at in range(side):
+        n_received(1 - core, at)
+        total = total + wrecv[1 - core, at].astype(f32)
+    wg_ref[...] = total
+
+    pair_copy(2, sret_in.at[core], sret_in.at[core]).wait_send()
+    pair_copy(3, aret_in.at[core], aret_in.at[core]).wait_send()
+    for shift in range(1, side):
+        m_copy(shift).wait_send()
+        for to_core in range(2):
+            n_copy(shift, to_core).wait_send()
+    n_copy(0, 1 - core).wait_send()
+    sent_all(r_copy, n_chip)
     if n_head > 1:
         for i in range(8):
             o_copy(i).wait_send()
@@ -592,6 +632,7 @@
 
 def per_device(n_ctx, n_head, queries, key_vectors, value_rows, write_rate, log_decay, doc_offsets, out_weight, grad_out):
     n_chip = n_ctx // 2
+    side = 4 if n_chip == 16 else 1
     tok, dim = queries.shape
     width = grad_out.shape[1]
     share = grad_out.shape[0]
@@ -605,23 +646,24 @@
         pltpu.VMEM((tok, dim), bf16), pltpu.VMEM((tok, dim), bf16), pltpu.VMEM((tok, 2 * dim), bf16),
         pltpu.VMEM((2, tok), f32), pltpu.VMEM((2, tok), f32), pltpu.VMEM((2 * dim, width), bf16),
         pltpu.VMEM((n_head, share, width), bf16),
-        pltpu.VMEM((n_head, n_chip, share, width // n_chip), bf16),
-        pltpu.VMEM((n_chip, width // n_chip, tok), bf16),
+        pltpu.VMEM((n_head, side, side, share, width // n_chip), bf16),
+        pltpu.VMEM((side * (width // n_chip), side * tok), bf16),
         pltpu.VMEM((2, 2, dim, dim), f32), pltpu.VMEM((2, 2, dim, dim), f32),
         pltpu.VMEM((2, dim, dim), f32), pltpu.VMEM((2, dim, dim), f32),
-        pltpu.VMEM((n_chip, dim, dim), f32), pltpu.VMEM((n_chip, tok, 2 * dim), bf16),
+        pltpu.VMEM((n_chip, dim, dim), f32), pltpu.VMEM((side, tok, 2 * dim), bf16),
         pltpu.VMEM((n_chip, sl, dim), f32), pltpu.VMEM((n_chip, sl, dim), f32),
         pltpu.VMEM((n_chip, sl, dim), f32), pltpu.VMEM((n_chip, sl, dim), f32),
         pltpu.VMEM((n_chip, sl, dim), f32), pltpu.VMEM((2, n_chip, sl, dim), f32),
         pltpu.VMEM((n_chip, sl, dim), f32), pltpu.VMEM((2, n_chip, sl, dim), f32),
         pltpu.VMEM((n_head, share, width), bf16), pltpu.VMEM((n_head, share, width), f32),
         pltpu.VMEM((2, share, width), bf16), pltpu.VMEM((8, share, width), bf16),
-        pltpu.VMEM((2, wrows, 2 * dim), f32), pltpu.VMEM((wrows, 2 * dim), f32),
+        pltpu.VMEM((side, 2, wrows, 2 * dim), f32), pltpu.VMEM((side, 2, wrows, 2 * dim), bf16),
+        pltpu.VMEM((2, side, wrows, 2 * dim), bf16),
         dma((8,)),
-        dma((8,)), dma((n_head, 2)), dma((n_chip,)), dma((n_chip,)), dma((8,)), dma((n_head, 2)), dma((3,)), dma((3,)),
-        dma((19,)), dma((n_chip, 2)), dma((19,)), dma((n_chip, 2)),
+        dma((8,)), dma((n_head, 2)), dma((n_chip,)), dma((n_chip,)), dma((8,)), dma((n_head, 2)), dma((4,)), dma((4,)),
+        dma((19,)), dma((n_chip, 2)), dma((side,)), dma((side,)), dma((side, 2)), dma((2, side)),
         dma((n_chip,)), dma((n_chip,)), dma((n_chip,)), dma((n_chip,)),
-        dma((n_ctx,)), dma((n_ctx,)), dma((n_ctx,)), dma((n_ctx,)), dma((8,)), dma((8,)),
+        dma((n_chip,)), dma((n_chip,)), dma((n_chip,)), dma((n_chip,)), dma((8,)), dma((8,)),
     ]
     shapes = (
         jax.ShapeDtypeStruct((share, width), f32),

time: 56.7 us -> 50.2 us (0.89)
  Pallas kernels: 55.9 us -> 49.5 us
    pallas_call x1, Pallas kernels: 54 us -> 47.6 us  [per_device(): pl.pallas_call(functools.partial(kernel, n_ctx, n_head), out_shape=shapes...]
where the time goes in v5:
time: 50.2 us; the launch traced here: 50.1 us
  Pallas kernels  49.5 us (99%)
  between operations  0.64 us (1%)
    pallas_call x1, Pallas kernels, per_device(): pl.pallas_call(functools.partial(kernel, n_ctx, n_head), out_shape=shapes...  47.6 us
    pallas_call x1, Pallas kernels, per_device(): pl.pallas_call(emit, out_shape=shapes, in_specs=[vmem] * 7, out_specs=(hb...  1.87 us

profile of v5, /device:TPU:1, one launch (start us, length us, event | category | flops | bytes accessed | tf_op | source)
XLA Modules:
  0.0 50.1 jit_solution(13480868852656806366)
XLA Ops:
  0.6 47.6 %layer.1 = (f32[16,2048]{1,0:T(8,128)}, f32[128,128]{1,0:T(8,128)}, f32[128,128]{1,0:T(8,128)}, f32[128,256]{1,0:T(8,128)}, f32[2,128]{1,0:T(2,128)}, /*index=5*/f32[2,128]{1,0:T(2,128)}, f32[64,256]{1,0:T(8,128)}) custom-call(s32[5]{0:T(128)} %docs_hbm.1, bf16[128,128]{1,0:T(8,128)(2,1)} %q_hbm.1, bf16[128,128]{1,0:T(8,128)(2,1)} %k_hbm.1, ...), custom_call_target="tpu_custom_call" | custom-call | tf_op jit(solution)/shard_map/layer/pallas_call | solution.py:677
  48.3 1.9 %emit.1 = (f32[16,2048]{1,0:T(8,128)}, f32[128,128]{1,0:T(8,128)}, f32[128,128]{1,0:T(8,128)}, f32[128,256]{1,0:T(8,128)}, f32[2,128]{1,0:T(2,128)}, /*index=5*/f32[2,128]{1,0:T(2,128)}, f32[64,256]{1,0:T(8,128)}) custom-call(f32[16,2048]{1,0:T(8,128)} %get-tuple-element.14.refs_0_, f32[128,128]{1,0:T(8,128)} %get-tuple-element.15.refs_1_, ...), custom_call_target="tpu_custom_call" | custom-call | tf_op jit(solution)/shard_map/emit/pallas_call | solution.py:687

commit v6 on v5

--- a/solution.py
+++ b/solution.py
@@ -112,7 +112,7 @@
         def copy(i, block, shift, half):
             ref = buf.at[block] if half is None else part(buf, block, half)
             return pltpu.make_async_remote_copy(
-                src_ref=ref, dst_ref=ref, send_sem=ss.at[i], recv_sem=rs.at[block, half or 0],
+                src_ref=ref, dst_ref=ref, send_sem=ss.at[0], recv_sem=rs.at[block, half or 0],
                 device_id=(c, zed(shift)), device_id_type=MESH)
 
         def start(*which):
@@ -132,8 +132,7 @@
             start(6, 7)
 
         def sent():
-            for i, (origin, shift, half) in enumerate(sends):
-                copy(i, zed(origin), shift, half).wait_send()
+            all_sent(buf.at[pl.ds(0, 7)], ss)
 
         return start, relay, received, sent
 
@@ -150,7 +149,7 @@
             block = chip_at(*origin)
             ref = buf.at[block] if half is None else buf.at[block, pl.ds(half * rows_of, rows_of)]
             return pltpu.make_async_remote_copy(
-                src_ref=ref, dst_ref=ref, send_sem=ss.at[i], recv_sem=rs.at[block, half or 0],
+                src_ref=ref, dst_ref=ref, send_sem=ss.at[0], recv_sem=rs.at[block, half or 0],
                 device_id=(chip_at(*to) * 2 + core, z), device_id_type=MESH)
 
         def start(origin, to, half=None):
@@ -184,8 +183,7 @@
                     received((shift, 2), half)
 
         def sent():
-            for i, args in enumerate(sends):
-                copy(i, *args).wait_send()
+            all_sent(buf.at[pl.ds(0, n_chip - 1)], ss)
 
         return own, first, second, last, sent
 
@@ -202,10 +200,18 @@
             src_ref=src, dst_ref=dst, send_sem=p_ss.at[i], recv_sem=p_rs.at[i],
             device_id=(partner, z), device_id_type=MESH)
 
+    def all_sent(ref, sem):
+        pltpu.make_async_remote_copy(src_ref=ref, dst_ref=ref, send_sem=sem.at[0], recv_sem=p_rs.at[0],
+                                     device_id=(partner, z), device_id_type=MESH).wait_send()
+
+    def all_received(ref, sem):
+        pltpu.make_async_remote_copy(src_ref=ref, dst_ref=ref, send_sem=p_ss.at[0], recv_sem=sem,
+                                     device_id=(partner, z), device_id_type=MESH).wait_recv()
+
     def to_chips(src_of, dst, ss, rs):
         def copy(i):
             return pltpu.make_async_remote_copy(
-                src_ref=src_of(peer(i)), dst_ref=dst, send_sem=ss.at[i], recv_sem=rs.at[i],
+                src_ref=src_of(peer(i)), dst_ref=dst, send_sem=ss.at[0], recv_sem=rs.at[0],
                 device_id=(peer(i) * 2 + core, z), device_id_type=MESH)
         return copy
 
@@ -221,24 +227,19 @@
         shift, second = lax.div(i, side), lax.rem(i, side)
         return pltpu.make_async_remote_copy(
             src_ref=gfull.at[z, :, columns(lax.rem(first_at + shift, side), second)],
-            dst_ref=gcol.at[z, first_at, second], send_sem=e_ss.at[i], recv_sem=e_rs.at[i],
+            dst_ref=gcol.at[z, first_at, second], send_sem=e_ss.at[0], recv_sem=e_rs.at[0],
             device_id=(chip_at(shift, 0) * 2 + core, z), device_id_type=MESH)
 
     def m_copy(shift):
         return pltpu.make_async_remote_copy(
-            src_ref=mall.at[first_at], dst_ref=mall.at[first_at], send_sem=m_ss.at[shift], recv_sem=m_rs.at[shift],
+            src_ref=mall.at[first_at], dst_ref=mall.at[first_at], send_sem=m_ss.at[0], recv_sem=m_rs.at[0],
             device_id=(chip_at(shift, 0) * 2 + core, z), device_id_type=MESH)
 
     def n_copy(shift, to_core):
         return pltpu.make_async_remote_copy(
             src_ref=wsend.at[lax.rem(second_at + shift, side), to_core], dst_ref=wrecv.at[core, second_at],
-            send_sem=n_ss.at[shift, to_core], recv_sem=n_rs.at[core, second_at],
+            send_sem=n_ss.at[0 if shift else 1], recv_sem=n_rs.at[core],
             device_id=(chip_at(0, shift) * 2 + to_core, z), device_id_type=MESH)
-
-    def n_received(of_core, at):
-        pltpu.make_async_remote_copy(
-            src_ref=wsend.at[0, 0], dst_ref=wrecv.at[of_core, at], send_sem=n_ss.at[0, 0],
-            recv_sem=n_rs.at[of_core, at], device_id=(partner, z), device_id_type=MESH).wait_recv()
 
     l_copy = to_chips(lambda to: lsend.at[to], lslice.at[chip], l_ss, l_rs)
     a_copy = to_chips(lambda to: asend.at[to], aslice.at[chip], a_ss, a_rs)
@@ -254,7 +255,7 @@
             part = pl.ds(half * (width // 2), width // 2)
             src, dst = lpart.at[zed(of), :, part], lrecv.at[i, :, part]
         return pltpu.make_async_remote_copy(
-            src_ref=src, dst_ref=dst, send_sem=o_ss.at[i], recv_sem=o_rs.at[i],
+            src_ref=src, dst_ref=dst, send_sem=o_ss.at[0], recv_sem=o_rs.at[i],
             device_id=(c, zed(to)), device_id_type=MESH)
 
     def start_all(copy, n, low=1):
@@ -420,7 +421,8 @@
             t_first(2)
     if n_head > 1:
         fence(g_relay)
-    recv_all(e_copy, n_chip, side)
+    if side > 1:
+        all_received(gcol.at[z, pl.ds(0, side - 1)], e_rs.at[0])
     if n_head > 1:
         fence(lambda: h_start(0, 1, 2, 3))
     if side > 1:
@@ -429,7 +431,8 @@
             t_second(1, 3)
             t_second(2)
             t_last()
-    recv_all(l_copy, n_chip)
+    if side > 1:
+        all_received(lslice.at[pl.ds(0, n_chip - 1)], l_rs.at[0])
     state = jnp.zeros((slice_rows, dim), f32)
     for i in range(n_chip):
         sret_out[i] = state
@@ -464,10 +467,12 @@
         fence(h_relay)
 
     tl_copy.wait_send()
-    t_sent()
-    sent_all(e_copy, n_chip, side)
-    sent_all(l_copy, n_chip)
-    recv_all(s_copy, n_chip)
+    if side > 1:
+        t_sent()
+        all_sent(gcol.at[0, pl.ds(0, side - 1)], e_ss)
+        all_sent(lsend.at[pl.ds(0, n_chip - 1)], l_ss)
+    if side > 1:
+        all_received(sret_in.at[core, pl.ds(0, n_chip - 1)], s_rs.at[0])
     fence(lambda: pair_copy(2, sret_in.at[core], sret_in.at[core]).start())
     pair_copy(2, sret_in.at[core], sret_in.at[1 - core]).wait_recv()
     mixed = []
@@ -492,7 +497,8 @@
                 o_copy(i).start()
     lfull[...] = partial
 
-    recv_all(a_copy, n_chip)
+    if side > 1:
+        all_received(aslice.at[pl.ds(0, n_chip - 1)], a_rs.at[0])
     adjoint = jnp.zeros((slice_rows, dim), f32)
     for j in reversed(range(n_chip)):
         aret_out[j] = adjoint
@@ -507,8 +513,7 @@
             gturn[second * chip_width:(second + 1) * chip_width, first_of * tok:(first_of + 1) * tok] = (
                 gcol[:, first_of, second].reshape(tok, chip_width).T)
     if side > 1:
-        for shift in (1, 3, 2):
-            m_copy(shift).wait_recv()
+        all_received(mall.at[pl.ds(0, side - 1)], m_rs.at[0])
     product = lax.dot_general(gturn[...], mall[...].reshape(side * tok, 2 * dim), (((1,), (0,)), ((), ())),
                               preferred_element_type=f32).reshape(wfull.shape)
     wsend[...] = product.astype(bf16)
@@ -554,13 +559,15 @@
     dq = dq + mm(dqks, ks)
     dk = mm(dqks, qs, 0, 0)
     gq_ref[...] = q_inv * (dq - qn * rowsum(qn * dq))
-    sent_all(s_copy, n_chip)
-    sent_all(a_copy, n_chip)
+    if side > 1:
+        all_sent(sret_out.at[pl.ds(0, n_chip - 1)], s_ss)
+        all_sent(asend.at[pl.ds(0, n_chip - 1)], a_ss)
     ap_copy.wait_send()
     if n_head > 1:
         g_sent()
         h_sent()
-    recv_all(r_copy, n_chip)
+    if side > 1:
+        all_received(aret_in.at[core, pl.ds(0, n_chip - 1)], r_rs.at[0])
     fence(lambda: pair_copy(3, aret_in.at[core], aret_in.at[core]).start())
     pair_copy(3, aret_in.at[core], aret_in.at[1 - core]).wait_recv()
     for h in range(2):
@@ -608,26 +615,25 @@
             result = result + lrecv[i].astype(f32)
     out_ref[...] = result
     total = wfull[second_at, core]
+    if side > 1:
+        all_received(wrecv.at[core, pl.ds(0, side - 1)], n_rs.at[core])
+    all_received(wrecv.at[1 - core], n_rs.at[1 - core])
     for shift in range(1, side):
         at = lax.rem(second_at + shift, side)
-        n_received(core, at)
         total = total + wrecv[core, at].astype(f32)
     for at in range(side):
-        n_received(1 - core, at)
         total = total + wrecv[1 - core, at].astype(f32)
     wg_ref[...] = total
 
     pair_copy(2, sret_in.at[core], sret_in.at[core]).wait_send()
     pair_copy(3, aret_in.at[core], aret_in.at[core]).wait_send()
-    for shift in range(1, side):
-        m_copy(shift).wait_send()
-        for to_core in range(2):
-            n_copy(shift, to_core).wait_send()
     n_copy(0, 1 - core).wait_send()
-    sent_all(r_copy, n_chip)
-    if n_head > 1:
-        for i in range(8):
-            o_copy(i).wait_send()
+    if side > 1:
+        all_sent(mall.at[pl.ds(0, side - 1)], m_ss)
+        all_sent(wsend.at[pl.ds(0, side - 1)], n_ss)
+        all_sent(aret_out.at[pl.ds(0, n_chip - 1)], r_ss)
+    if n_head > 1:
+        all_sent(lrecv.at[pl.ds(0, 7)], o_ss)
 
 
 def per_device(n_ctx, n_head, queries, key_vectors, value_rows, write_rate, log_decay, doc_offsets, out_weight, grad_out):
@@ -660,10 +666,10 @@
         pltpu.VMEM((side, 2, wrows, 2 * dim), f32), pltpu.VMEM((side, 2, wrows, 2 * dim), bf16),
         pltpu.VMEM((2, side, wrows, 2 * dim), bf16),
         dma((8,)),
-        dma((8,)), dma((n_head, 2)), dma((n_chip,)), dma((n_chip,)), dma((8,)), dma((n_head, 2)), dma((4,)), dma((4,)),
-        dma((19,)), dma((n_chip, 2)), dma((side,)), dma((side,)), dma((side, 2)), dma((2, side)),
-        dma((n_chip,)), dma((n_chip,)), dma((n_chip,)), dma((n_chip,)),
-        dma((n_chip,)), dma((n_chip,)), dma((n_chip,)), dma((n_chip,)), dma((8,)), dma((8,)),
+        dma((1,)), dma((n_head, 2)), dma((1,)), dma((1,)), dma((1,)), dma((n_head, 2)), dma((4,)), dma((4,)),
+        dma((1,)), dma((n_chip, 2)), dma((1,)), dma((1,)), dma((2,)), dma((2,)),
+        dma((1,)), dma((1,)), dma((1,)), dma((1,)),
+        dma((1,)), dma((1,)), dma((1,)), dma((1,)), dma((1,)), dma((8,)),
     ]
     shapes = (
         jax.ShapeDtypeStruct((share, width), f32),

time: 50.2 us -> 48.2 us (0.960)
  Pallas kernels: 49.5 us -> 47.5 us
    pallas_call x1, Pallas kernels: 47.6 us -> 45.6 us  [per_device(): pl.pallas_call(functools.partial(kernel, n_ctx, n_head), out_shape=shapes...]
where the time goes in v6:
time: 48.2 us; the launch traced here: 48.1 us
  Pallas kernels  47.5 us (99%)
  between operations  0.64 us (1%)
    pallas_call x1, Pallas kernels, per_device(): pl.pallas_call(functools.partial(kernel, n_ctx, n_head), out_shape=shapes...  45.6 us
    pallas_call x1, Pallas kernels, per_device(): pl.pallas_call(emit, out_shape=shapes, in_specs=[vmem] * 7, out_specs=(hb...  1.87 us

profile of v6, /device:TPU:1, one launch (start us, length us, event | category | flops | bytes accessed | tf_op | source)
XLA Modules:
  0.0 48.1 jit_solution(7700417114836137178)
XLA Ops:
  0.6 45.6 %layer.1 = (f32[16,2048]{1,0:T(8,128)}, f32[128,128]{1,0:T(8,128)}, f32[128,128]{1,0:T(8,128)}, f32[128,256]{1,0:T(8,128)}, f32[2,128]{1,0:T(2,128)}, /*index=5*/f32[2,128]{1,0:T(2,128)}, f32[64,256]{1,0:T(8,128)}) custom-call(s32[5]{0:T(128)} %docs_hbm.1, bf16[128,128]{1,0:T(8,128)(2,1)} %q_hbm.1, bf16[128,128]{1,0:T(8,128)(2,1)} %k_hbm.1, ...), custom_call_target="tpu_custom_call" | custom-call | tf_op jit(solution)/shard_map/layer/pallas_call | solution.py:683
  46.2 1.9 %emit.1 = (f32[16,2048]{1,0:T(8,128)}, f32[128,128]{1,0:T(8,128)}, f32[128,128]{1,0:T(8,128)}, f32[128,256]{1,0:T(8,128)}, f32[2,128]{1,0:T(2,128)}, /*index=5*/f32[2,128]{1,0:T(2,128)}, f32[64,256]{1,0:T(8,128)}) custom-call(f32[16,2048]{1,0:T(8,128)} %get-tuple-element.14.refs_0_, f32[128,128]{1,0:T(8,128)} %get-tuple-element.15.refs_1_, ...), custom_call_target="tpu_custom_call" | custom-call | tf_op jit(solution)/shard_map/emit/pallas_call | solution.py:693

commit v7 on v6

--- a/solution.py
+++ b/solution.py
@@ -93,8 +93,8 @@
         pl.semaphore_signal(barrier, inc=1, device_id=(lax.rem(c + i, n_ctx), z), device_id_type=MESH)
         return carry
 
-    lax.fori_loop(1, n_head, greet_head, 0)
-    lax.fori_loop(1, n_ctx, greet_ctx, 0)
+    lax.fori_loop(1, n_ctx, greet_ctx, 0, unroll=True)
+    lax.fori_loop(1, n_head, greet_head, 0, unroll=True)
 
     def zed(shift):
         return lax.rem(z + shift + n_head, n_head)
@@ -112,7 +112,7 @@
         def copy(i, block, shift, half):
             ref = buf.at[block] if half is None else part(buf, block, half)
             return pltpu.make_async_remote_copy(
-                src_ref=ref, dst_ref=ref, send_sem=ss.at[0], recv_sem=rs.at[block, half or 0],
+                src_ref=ref, dst_ref=ref, send_sem=ss.at[0], recv_sem=rs.at[block],
                 device_id=(c, zed(shift)), device_id_type=MESH)
 
         def start(*which):
@@ -122,8 +122,7 @@
 
         def received(*origins):
             for origin in origins:
-                for half in ((0, 1) if origin == 4 else (None,)):
-                    copy(0, zed(origin), 1, half).wait_recv()
+                copy(0, zed(origin), 1, None).wait_recv()
 
         def relay():
             received(-2)
@@ -149,7 +148,7 @@
             block = chip_at(*origin)
             ref = buf.at[block] if half is None else buf.at[block, pl.ds(half * rows_of, rows_of)]
             return pltpu.make_async_remote_copy(
-                src_ref=ref, dst_ref=ref, send_sem=ss.at[0], recv_sem=rs.at[block, half or 0],
+                src_ref=ref, dst_ref=ref, send_sem=ss.at[0], recv_sem=rs.at[block],
                 device_id=(chip_at(*to) * 2 + core, z), device_id_type=MESH)
 
         def start(origin, to, half=None):
@@ -179,8 +178,7 @@
 
         def last():
             for shift in (0, 1, 3, 2):
-                for half in range(2):
-                    received((shift, 2), half)
+                received((shift, 2))
 
         def sent():
             all_sent(buf.at[pl.ds(0, n_chip - 1)], ss)
@@ -262,19 +260,7 @@
         def body(i, carry):
             copy(i).start()
             return carry
-        lax.fori_loop(low, n, body, 0)
-
-    def recv_all(copy, n, low=1):
-        def body(i, carry):
-            copy(i).wait_recv()
-            return carry
-        lax.fori_loop(low, n, body, 0)
-
-    def sent_all(copy, n, low=1):
-        def body(i, carry):
-            copy(i).wait_send()
-            return carry
-        lax.fori_loop(low, n, body, 0)
+        lax.fori_loop(low, n, body, 0, unroll=True)
 
     for load in loads[1:6]:
         load.wait()
@@ -411,6 +397,7 @@
         t = info[h]
         through = mm(t["qts"], rows(tl_oth[h, 0], tl_oth[h, 1]), 1, 1)
         t["qfs"] = split(jnp.where(is_first, t["qt"], through[:, :dim]))
+        t["mes"] = split(mm(t["ms"], t["eks"], 0, 0))
         t["of"] = t["o"] + jnp.where(is_first, 0.0, through[:, dim:])
 
     if side > 1:
@@ -454,6 +441,8 @@
         a_own[h] = mm(t["dos"], t["qts"], 0, 0)
     ap_copy = pair_copy(1, a_own, a_oth)
     fence(lambda: pair_copy(1, a_own, a_oth).start())
+    if n_head > 1:
+        fence(h_relay)
 
     for h in range(2):
         t = info[h]
@@ -463,8 +452,6 @@
     asend[...] = (mm(a1, t0, 1, 1) + a0).reshape(n_chip, slice_rows, dim)
     start_all(a_copy, n_chip)
     aslice[chip] = asend[chip]
-    if n_head > 1:
-        fence(h_relay)
 
     tl_copy.wait_send()
     if side > 1:
@@ -551,8 +538,7 @@
         t["pps"] = split(t["p"])
         t["xp"] = mm(t["dos"], t["pps"], 1, 1) * t["ratio"]
         t["d_o_s"] = mm(t["dos"], t["ss"])
-        turned = mm(t["ms"], cols(t["pd"], t["eks"]), 0, 0)
-        t["dr0"], t["mes"] = turned[:, :dim], split(turned[:, dim:])
+        t["dr0"] = mm(t["ms"], t["pd"], 0, 0)
         dqk = dqk + t["xp"]
         dq = dq + t["f"] * t["d_o_s"]
     dqks = split(dqk)
@@ -666,8 +652,8 @@
         pltpu.VMEM((side, 2, wrows, 2 * dim), f32), pltpu.VMEM((side, 2, wrows, 2 * dim), bf16),
         pltpu.VMEM((2, side, wrows, 2 * dim), bf16),
         dma((8,)),
-        dma((1,)), dma((n_head, 2)), dma((1,)), dma((1,)), dma((1,)), dma((n_head, 2)), dma((4,)), dma((4,)),
-        dma((1,)), dma((n_chip, 2)), dma((1,)), dma((1,)), dma((2,)), dma((2,)),
+        dma((1,)), dma((n_head,)), dma((1,)), dma((1,)), dma((1,)), dma((n_head,)), dma((4,)), dma((4,)),
+        dma((1,)), dma((n_chip,)), dma((1,)), dma((1,)), dma((2,)), dma((2,)),
         dma((1,)), dma((1,)), dma((1,)), dma((1,)),
         dma((1,)), dma((1,)), dma((1,)), dma((1,)), dma((1,)), dma((8,)),
     ]

time: 48.2 us -> 48.1 us (level)
  no operation moved by 1% of the time
where the time goes in v7:
time: 48.1 us; the launch traced here: 48 us
  Pallas kernels  47.4 us (99%)
  between operations  0.64 us (1%)
    pallas_call x1, Pallas kernels, per_device(): pl.pallas_call(functools.partial(kernel, n_ctx, n_head), out_shape=shapes...  45.5 us
    pallas_call x1, Pallas kernels, per_device(): pl.pallas_call(emit, out_shape=shapes, in_specs=[vmem] * 7, out_specs=(hb...  1.87 us

profile of v7, /device:TPU:1, one launch (start us, length us, event | category | flops | bytes accessed | tf_op | source)
XLA Modules:
  0.0 48.0 jit_solution(7109221943794559551)
XLA Ops:
  0.6 45.5 %layer.1 = (f32[16,2048]{1,0:T(8,128)}, f32[128,128]{1,0:T(8,128)}, f32[128,128]{1,0:T(8,128)}, f32[128,256]{1,0:T(8,128)}, f32[2,128]{1,0:T(2,128)}, /*index=5*/f32[2,128]{1,0:T(2,128)}, f32[64,256]{1,0:T(8,128)}) custom-call(s32[5]{0:T(128)} %docs_hbm.1, bf16[128,128]{1,0:T(8,128)(2,1)} %q_hbm.1, bf16[128,128]{1,0:T(8,128)(2,1)} %k_hbm.1, ...), custom_call_target="tpu_custom_call" | custom-call | tf_op jit(solution)/shard_map/layer/pallas_call | solution.py:669
  46.1 1.9 %emit.1 = (f32[16,2048]{1,0:T(8,128)}, f32[128,128]{1,0:T(8,128)}, f32[128,128]{1,0:T(8,128)}, f32[128,256]{1,0:T(8,128)}, f32[2,128]{1,0:T(2,128)}, /*index=5*/f32[2,128]{1,0:T(2,128)}, f32[64,256]{1,0:T(8,128)}) custom-call(f32[16,2048]{1,0:T(8,128)} %get-tuple-element.14.refs_0_, f32[128,128]{1,0:T(8,128)} %get-tuple-element.15.refs_1_, ...), custom_call_target="tpu_custom_call" | custom-call | tf_op jit(solution)/shard_map/emit/pallas_call | solution.py:679
